TPU v7x, 128 devices: a whole 4x4x4 slice. The times are simulated.
128 devices in a mesh: basis: 64 (over z, y, x), ex: 2 (over core).
Axes of the slice: x: 4, y: 4, z: 4, core: 2. Of those that a mesh axis runs over, the one named last changes fastest.
Arguments:
- activations: bfloat16 [256, 768, 2880], P(('basis', 'ex')), may hold values from -6 to 6
- out_grads: bfloat16 [256, 768, 2880], P(('basis', 'ex')), may hold values from -0.25 to 0.25
- grad_basis: bfloat16 [2880, 256], replicated, may hold values from -0.109375 to 0.109375
- panel_store: bfloat16 [64, 4, 2880, 128], P('basis', None, 'ex'), may hold values from -0.109375 to 0.109375
- owners: int32 [4], replicated, may hold values from 0 to 63, as said below
- token_count: int32 [256], P(('basis', 'ex')), may hold values from 96 to 768, as said below
Outputs:
- scaled: float32 [256, 256, 512], P('basis', 'ex')
Inputs may be any that keep to these rules, and one draw needn't show every extreme that they name: `owners`: values are basis indices; panels may share an owner. `token_count`: some example has all 768 tokens live.
All inputs are finite; a program needn't handle non-finite values.
Results may differ from a plain program's by a relative error of at most 0.00045.
The roundings to bfloat16 on the way count: a program that leaves them out, or rounds other values in their place, can miss the bound.
Values may be sent and summed in bfloat16 or wider, within the bound.
No kernel may reach another device: no remote copies, remote signals or barrier semaphores. Data moves between devices by JAX's collectives and lax.ppermute only.
A program may use at most 128 MiB of HBM per device.

v0:
```python
import jax
import jax.numpy as jnp
from jax import lax
from jax.experimental import pallas as pl
from jax.experimental.pallas import tpu as pltpu
from jax.sharding import PartitionSpec as P

ROWS = 48
TT = 256
HALF = 1440
F32 = jnp.float32
BF16 = jnp.bfloat16


def in_vmem(n):
    return [pl.BlockSpec(memory_space=pltpu.VMEM)] * n


def turn_kernel(x_ref, o_ref):
    o_ref[0] = x_ref[0].T


def turned(activations):
    local, tok, width = activations.shape
    x = pltpu.with_memory_space_constraint(jnp.swapaxes(activations, 1, 2), pltpu.HBM)
    return pl.pallas_call(
        turn_kernel,
        grid=(local,),
        in_specs=[pl.BlockSpec((1, width, tok), lambda n: (n, 0, 0))],
        out_specs=pl.BlockSpec((1, tok, width), lambda n: (n, 0, 0)),
        out_shape=pltpu.HBM((local, tok, width), BF16),
        compiler_params=pltpu.CompilerParams(vmem_limit_bytes=28 << 20),
        cost_estimate=pl.CostEstimate(flops=0, transcendentals=0, bytes_accessed=4 * local * tok * width),
    )(x)


def pair_of_panels(ref):
    half = HALF
    blocks = half // ROWS
    cols = []
    for k in range(2):
        rows = [ref[pl.ds(k * blocks, blocks), h].reshape(half, 128) for h in range(2)]
        cols.append(jnp.concatenate(rows, axis=0))
    return jnp.concatenate(cols, axis=1)


def pair_products(act_ref, rg_ref, basis_ref, rot):
    local, tok, _ = act_ref.shape
    pair = pair_of_panels(basis_ref)
    for n in range(local):
        for t in range(0, tok, TT):
            rows = pl.ds(t, TT)
            rot[n, rows] = jnp.dot(act_ref[n, rows], pair, preferred_element_type=F32).astype(BF16)
    return [jnp.dot(rg_ref[n], rot[n], preferred_element_type=F32) for n in range(local)]


def first_kernel(act_ref, rg_ref, basis_ref, ex_ref, rot):
    for n, ex in enumerate(pair_products(act_ref, rg_ref, basis_ref, rot)):
        ex_ref[n] = ex


def second_kernel(e_ref, act_ref, rg_ref, basis_ref, own_ref, keep_ref, send_ref, sq_ref, rot, ex_ref, sq):
    e = e_ref[0]
    local, dirs, cols = own_ref.shape
    mid = dirs // 2
    for n, ex in enumerate(pair_products(act_ref, rg_ref, basis_ref, rot)):
        ex_ref[n] = ex
    here, there = (pl.ds(pl.multiple_of(x * mid, 8), mid) for x in (e, 1 - e))
    for n in range(local):
        for side, src in enumerate((own_ref, ex_ref)):
            keep_ref[n, side] = src[n, here, :]
            send_ref[n, side] = src[n, there, :]
    for side, src in enumerate((own_ref, ex_ref)):
        pair = e if side == 0 else 1 - e
        for h in range(2):
            for r in range(mid // 8):
                for c in range(cols // 128):
                    at = (pl.ds(h * mid + 8 * r, 8), pl.ds(128 * c, 128))
                    tile = src[0, at[0], at[1]] * src[0, at[0], at[1]]
                    for n in range(1, local):
                        tile += src[n, at[0], at[1]] * src[n, at[0], at[1]]
                    sq_ref[2 * (2 * (cols // 128) * r + (cols // 128) * pair + c) + h] = tile


def ex_gradients(e, act, rg, mine, other):
    local, tok, width = act.shape
    dirs = rg.shape[1]
    cost = pl.CostEstimate(
        flops=2 * local * tok * width * 256, transcendentals=0, bytes_accessed=2 * local * tok * width
    )
    own = pl.pallas_call(
        first_kernel,
        in_specs=in_vmem(3),
        out_specs=pl.BlockSpec(memory_space=pltpu.VMEM),
        out_shape=pltpu.VMEM((local, dirs, 256), F32),
        scratch_shapes=[pltpu.VMEM((local, tok, 256), BF16)],
        compiler_params=pltpu.CompilerParams(vmem_limit_bytes=16 << 20),
        cost_estimate=cost,
    )(act, rg, mine)
    return pl.pallas_call(
        second_kernel,
        in_specs=[pl.BlockSpec(memory_space=pltpu.SMEM)] + in_vmem(4),
        out_specs=in_vmem(3),
        out_shape=[
            pltpu.HBM((local, 2, dirs // 2, 256), F32),
            pltpu.HBM((local, 2, dirs // 2, 256), F32),
            pltpu.HBM((dirs * 512 // 1024, 8, 128), F32),
        ],
        scratch_shapes=[
            pltpu.VMEM((local, tok, 256), BF16),
            pltpu.VMEM((local, dirs, 256), F32),
            pltpu.VMEM((dirs, 256), F32),
        ],
        compiler_params=pltpu.CompilerParams(vmem_limit_bytes=16 << 20),
        cost_estimate=cost,
    )(e, act, rg, other, own)


def scale_kernel(e_ref, lam_ref, keep_ref, got_ref, o_ref, inv):
    e, i = e_ref[0], pl.program_id(0)
    local = keep_ref.shape[0]
    tiles, across = lam_ref.shape[0] // 2, 4

    @pl.when(i == 0)
    def _():
        damp = jnp.sum(jnp.sum(lam_ref[...], axis=0), keepdims=True) * (0.1 / lam_ref.size)
        for j in range(tiles):
            r, c = j // across, j % across
            inv[pl.ds(8 * r, 8), pl.ds(128 * c, 128)] = 1.0 / (lam_ref[2 * j + e] + damp)

    for core in range(2):
        for j in range(local):
            for own in range(2):

                @pl.when((i == core * local + j) & (own == (e == core)))
                def _():
                    src = keep_ref if own else got_ref
                    for side in range(2):
                        at = pl.ds(256 * (core if side == 0 else 1 - core), 256)
                        o_ref[0, :, at] = src[j, side] * inv[:, at]


def scaled_rows(e, lam, keep, got):
    local, _, dirs, _ = keep.shape

    def whole(x):
        return pl.BlockSpec(x.shape, lambda i, e: (0,) * x.ndim)

    return pl.pallas_call(
        scale_kernel,
        grid_spec=pltpu.PrefetchScalarGridSpec(
            num_scalar_prefetch=1,
            grid=(2 * local,),
            in_specs=[whole(lam), whole(keep), whole(got)],
            out_specs=pl.BlockSpec((1, dirs, 512), lambda i, e: (i, 0, 0)),
            scratch_shapes=[pltpu.VMEM((dirs, 512), F32)],
        ),
        out_shape=jax.ShapeDtypeStruct((2 * local, dirs, 512), F32),
        compiler_params=pltpu.CompilerParams(vmem_limit_bytes=8 << 20),
    )(e, lam, keep, got)


def per_device(activations, out_grads, grad_basis, panel_store, owners, token_count):
    local, tok, width = activations.shape
    _, panels, half, pw = panel_store.shape
    n_basis, n_ex = lax.axis_size("basis"), lax.axis_size("ex")
    b, e = lax.axis_index("basis"), lax.axis_index("ex")
    e1 = e.reshape(1).astype(jnp.int32)
    blocks = half // ROWS
    pairs = panels // 2

    slots = panel_store.reshape(pairs, 2 * blocks, ROWS, pw)
    slots = jnp.pad(slots, ((0, 0), (0, n_basis - 2 * blocks), (0, 0), (0, 0)))
    arrived = lax.all_to_all(slots.reshape(pairs * n_basis, ROWS, pw), ("ex", "basis"), 0, 0, tiled=True)
    act = turned(activations)
    rg = lax.dot_general(grad_basis, out_grads, (((0,), (2,)), ((), ())), preferred_element_type=F32)
    rg = jnp.transpose(rg, (1, 0, 2)).astype(BF16)
    live = jnp.arange(tok)[None, :] < token_count[:, None]
    rg = jnp.where(live[:, None, :], rg, jnp.zeros((), BF16))
    arrived, act, rg = lax.optimization_barrier((arrived, act, rg))

    owner = owners[2 * e + jnp.where(b < blocks, 0, 1)]
    block = lax.dynamic_index_in_dim(arrived.reshape(2, n_basis, ROWS, pw), owner, 1, keepdims=False)
    spread = jnp.broadcast_to(block[None], (n_basis, 2, ROWS, pw))
    mine = lax.all_to_all(spread, "basis", 0, 0, tiled=True)

    swap = [(0, 1), (1, 0)]
    other = lax.ppermute(mine, "ex", swap)
    keep, send, squares = ex_gradients(e1, act, rg, mine, other)
    got = lax.ppermute(send, "ex", swap)
    both = ("basis", "ex")
    parts = lax.all_to_all(squares, both, 0, 0, tiled=True)
    lam = jnp.sum(parts, axis=0, keepdims=True) * (1.0 / (local * n_basis * n_ex))
    lam = lax.all_to_all(jnp.broadcast_to(lam, parts.shape), both, 0, 0, tiled=True)
    return scaled_rows(e1, lam, keep, got)


def solution(mesh):
    return jax.shard_map(
        per_device,
        mesh=mesh,
        in_specs=(
            P(("basis", "ex"), None, None),
            P(("basis", "ex"), None, None),
            P(),
            P("basis", None, "ex", None),
            P(),
            P(("basis", "ex")),
        ),
        out_specs=P("basis", "ex", None),
        check_vma=False,
    )
```

profile of v0, /device:TPU:1, one launch (start us, length us, event | category | flops | bytes accessed | tf_op | source)
XLA Modules:
  0.0 119.2 jit_solution(6225599129660697913)
XLA Ops:
  0.0 0.0 copy-start
  0.0 2.7 %pad.4 = bf16[2,64,48,128]{3,2,1,0:T(8,128)(2,1)} pad(bf16[2,60,48,128]{3,2,1,0:T(8,128)(2,1)} %bitcast.21, bf16[]{:T(256)} %constant.12.clone.1), padding=0_0x0_4x0_0x0_0 | pad | bytes 3047426 | tf_op jit(solution)/shard_map/jit(_pad)/pad | solution.py:173
  2.7 11.9 %all-to-all-start = ((bf16[128,48,128]{2,1,0:T(8,128)(2,1)}), bf16[128,48,128]{2,1,0:T(8,128)(2,1)}, u32[]{:S(2)}, u32[]{:S(2)}) async-start(bf16[128,48,128]{2,1,0:T(8,128)(2,1)} %bitcast.2), calls=%async_computation | async-start | bytes 3145728 | tf_op jit(solution)/shard_map/all_to_all | solution.py:174
  14.6 0.0 copy-start.4
  14.6 0.0 copy-start.3
  14.7 7.0 %shard_map.64.act_ref = bf16[2,768,2880]{2,1,0:T(8,128)(2,1)} custom-call(bf16[2,2880,768]{2,1,0:T(8,128)(2,1)} %bitcast.20), custom_call_target="tpu_custom_call" | custom-call | bytes 17694720 | tf_op jit(solution)/shard_map/pallas_call | solution.py:26
  21.6 0.0 copy-done.4
  21.6 0.6 dynamic_slice.7
  24.2 0.0 copy-done.3
  24.2 0.1 iota_compare_fusion
  24.3 0.0 copy-done
  24.3 6.1 %fusion.8.rg_ref = bf16[2,256,768]{2,1,0:T(8,128)(2,1)S(1)} fusion(bf16[2,768,2880]{1,2,0:T(8,128)(2,1)} %param.7, bf16[2880,256]{1,0:T(8,128)(2,1)S(1)} %copy-done, pred[2,768]{1,0:T(4,128)(4,1)S(1)} %iota_compare_fusion), kind=kOutput, calls=%fused_computation.4 | convolution fusion | flops 2265710592 | bytes 11109888 | tf_op jit(solution)/shard_map/dot_general | solution.py:176
  30.4 7.3 %all-to-all-done = bf16[128,48,128]{2,1,0:T(8,128)(2,1)} async-done(((bf16[128,48,128]{2,1,0:T(8,128)(2,1)}), bf16[128,48,128]{2,1,0:T(8,128)(2,1)}, u32[]{:S(2)}, u32[]{:S(2)}) %all-to-all-start) | async-done | bytes 1572896 | tf_op jit(solution)/shard_map/all_to_all | solution.py:174
  37.7 0.7 dynamic-slice_bitcast_fusion
  38.4 0.2 broadcast_in_dim.32
  38.6 29.3 %all_to_all.20.basis_ref = bf16[64,2,48,128]{3,2,1,0:T(8,128)(2,1)S(1)} all-to-all(bf16[64,2,48,128]{3,2,1,0:T(8,128)(2,1)S(1)} %broadcast_in_dim.32), channel_id=1, replica_groups=mesh['basis'=64,'ex'=2] {'basis'}, dimensions={0} | all-to-all | bytes 3145728 | tf_op jit(solution)/shard_map/all_to_all | solution.py:185
  67.9 2.1 %collective-permute-start = (bf16[64,2,48,128]{3,2,1,0:T(8,128)(2,1)S(1)}, bf16[64,2,48,128]{3,2,1,0:T(8,128)(2,1)S(1)}, u32[]{:S(2)}, u32[]{:S(2)}) collective-permute-start(bf16[64,2,48,128]{3,2,1,0:T(8,128)(2,1)S(1)} %all_to_all.20.basis_ref), channel_id=1, source_target_pairs={{0,1},{1,0},{2,3},{3,2},{4,5},{5,4},{6,7},{7,6},{8,9},{9,8},{10,11... | collective-permute-start | bytes 4718600 | tf_op jit(solution)/shard_map/ppermute | solution.py:188
  70.0 0.0 copy-start.1
  70.0 3.6 %copy-done.1 = bf16[2,768,2880]{2,1,0:T(8,128)(2,1)S(1)} copy-done((bf16[2,768,2880]{2,1,0:T(8,128)(2,1)S(1)}, bf16[2,768,2880]{2,1,0:T(8,128)(2,1)}, u32[]{:S(2)}) %copy-start.1) | copy-done | bytes 8847384
  73.6 2.8 %shard_map.65.own_ref = f32[2,256,256]{2,1,0:T(8,128)S(1)} custom-call(bf16[2,768,2880]{2,1,0:T(8,128)(2,1)S(1)} %copy-done.1, bf16[2,256,768]{2,1,0:T(8,128)(2,1)S(1)} %fusion.8.rg_ref, bf16[64,2,48,128]{3,2,1,0:T(8,128)(2,1)S(1)} %all_to_all.20.basis_ref), custom_call_target="tpu_custom_call" | custom-call | flops 2264924160 | bytes 8847360 | tf_op jit(solution)/shard_map/pallas_call | solution.py:91
  76.4 0.0 collective-permute-done.basis_ref
  76.4 4.0 %shard_map.66 = (f32[2,2,128,256]{3,2,1,0:T(8,128)}, f32[2,2,128,256]{3,2,1,0:T(8,128)}, f32[128,8,128]{2,1,0:T(8,128)}) custom-call(s32[1]{0:T(128)} %bitcast.e_ref, bf16[2,768,2880]{2,1,0:T(8,128)(2,1)S(1)} %copy-done.1, bf16[2,256,768]{2,1,0:T(8,128)(2,1)S(1)} %fusion.8.rg_ref, bf16[64,2,48,128]{3,2,1,0:T(8,128)(2,1)S(1)} %collective-permute-done.basis_ref, ...), custom_call_target="tpu_custom_call" | custom-call | flops 2264924160 | bytes 8847360 | tf_op jit(solution)/shard_map/pallas_call | solution.py:100
  80.4 3.9 %all-to-all-start.2 = ((f32[128,8,128]{2,1,0:T(8,128)}), f32[128,8,128]{2,1,0:T(8,128)S(1)}, u32[]{:S(2)}, u32[]{:S(2)}) async-start(f32[128,8,128]{2,1,0:T(8,128)} %get-tuple-element.14), calls=%async_computation.2 | async-start | bytes 1048576 | tf_op jit(solution)/shard_map/all_to_all | solution.py:192
  84.3 1.1 collective-permute-start.1
  85.5 12.6 %all-to-all-done.2 = f32[128,8,128]{2,1,0:T(8,128)S(1)} async-done(((f32[128,8,128]{2,1,0:T(8,128)}), f32[128,8,128]{2,1,0:T(8,128)S(1)}, u32[]{:S(2)}, u32[]{:S(2)}) %all-to-all-start.2) | async-done | bytes 524320 | tf_op jit(solution)/shard_map/all_to_all | solution.py:192
  98.1 0.1 reduce_sum.9
  98.2 0.8 broadcast_in_dim.33
  99.0 4.5 %all-to-all-start.3 = ((f32[128,8,128]{2,1,0:T(8,128)}), f32[128,8,128]{2,1,0:T(8,128)S(1)}, u32[]{:S(2)}, u32[]{:S(2)}) async-start(f32[128,8,128]{2,1,0:T(8,128)} %broadcast_in_dim.33), calls=%async_computation.3 | async-start | bytes 1048576 | tf_op jit(solution)/shard_map/all_to_all | solution.py:194
  103.6 0.0 collective-permute-done.1.got_ref
  103.6 13.7 %all-to-all-done.3.lam_ref = f32[128,8,128]{2,1,0:T(8,128)S(1)} async-done(((f32[128,8,128]{2,1,0:T(8,128)}), f32[128,8,128]{2,1,0:T(8,128)S(1)}, u32[]{:S(2)}, u32[]{:S(2)}) %all-to-all-start.3) | async-done | bytes 524320 | tf_op jit(solution)/shard_map/all_to_all | solution.py:194
  117.3 0.0 copy-done.2
  117.3 1.9 %shard_map.67 = f32[4,128,512]{2,1,0:T(8,128)} custom-call(s32[1]{0:T(128)} %bitcast.e_ref, f32[128,8,128]{2,1,0:T(8,128)S(1)} %all-to-all-done.3.lam_ref, f32[2,2,128,256]{3,2,1,0:T(8,128)S(1)} %copy-done.2, f32[2,2,128,256]{3,2,1,0:T(8,128)S(1)} %collective-permute-done.1.got_ref), custom_call_target="tpu_custom_call" | custom-call | tf_op jit(solution)/shard_map/pallas_call | solution.py:149
  (2 shorter events, 0.0 us)
Async XLA Ops:
  0.0 24.3 %copy-start = (bf16[2880,256]{1,0:T(8,128)(2,1)S(1)}, bf16[2880,256]{1,0:T(8,128)(2,1)}, u32[]{:S(2)}) copy-start(bf16[2880,256]{1,0:T(8,128)(2,1)} %param.8) | copy-start | bytes 4423684
  2.7 34.9 %all-to-all-start = ((bf16[128,48,128]{2,1,0:T(8,128)(2,1)}), bf16[128,48,128]{2,1,0:T(8,128)(2,1)}, u32[]{:S(2)}, u32[]{:S(2)}) async-start(bf16[128,48,128]{2,1,0:T(8,128)(2,1)} %bitcast.2), calls=%async_computation | async-start | bytes 3145728 | tf_op jit(solution)/shard_map/all_to_all | solution.py:174
  14.6 7.0 %copy-start.4 = (s32[4]{0:T(128)S(1)}, s32[4]{0:T(128)}, u32[]{:S(2)}) copy-start(s32[4]{0:T(128)} %param.10) | copy-start | bytes 52
  14.6 9.5 %copy-start.3 = (s32[2]{0:T(128)S(1)}, s32[2]{0:T(128)}, u32[]{:S(2)}) copy-start(s32[2]{0:T(128)} %param.11) | copy-start | bytes 28
  67.9 8.5 %collective-permute-start = (bf16[64,2,48,128]{3,2,1,0:T(8,128)(2,1)S(1)}, bf16[64,2,48,128]{3,2,1,0:T(8,128)(2,1)S(1)}, u32[]{:S(2)}, u32[]{:S(2)}) collective-permute-start(bf16[64,2,48,128]{3,2,1,0:T(8,128)(2,1)S(1)} %all_to_all.20.basis_ref), channel_id=1, source_target_pairs={{0,1},{1,0},{2,3},{3,2},{4,5},{5,4},{6,7},{7,6},{8,9},{9,8},{10,11... | collective-permute-start | bytes 4718600 | tf_op jit(solution)/shard_map/ppermute | solution.py:188
  70.0 3.6 %copy-start.1 = (bf16[2,768,2880]{2,1,0:T(8,128)(2,1)S(1)}, bf16[2,768,2880]{2,1,0:T(8,128)(2,1)}, u32[]{:S(2)}) copy-start(bf16[2,768,2880]{2,1,0:T(8,128)(2,1)} %shard_map.64.act_ref) | copy-start | bytes 26542084
  80.4 36.8 %copy-start.2 = (f32[2,2,128,256]{3,2,1,0:T(8,128)S(1)}, f32[2,2,128,256]{3,2,1,0:T(8,128)}, u32[]{:S(2)}) copy-start(f32[2,2,128,256]{3,2,1,0:T(8,128)} %get-tuple-element.15.keep_ref) | copy-start | bytes 1572868
  80.4 17.6 %all-to-all-start.2 = ((f32[128,8,128]{2,1,0:T(8,128)}), f32[128,8,128]{2,1,0:T(8,128)S(1)}, u32[]{:S(2)}, u32[]{:S(2)}) async-start(f32[128,8,128]{2,1,0:T(8,128)} %get-tuple-element.14), calls=%async_computation.2 | async-start | bytes 1048576 | tf_op jit(solution)/shard_map/all_to_all | solution.py:192
  84.3 19.2 %collective-permute-start.1 = (f32[2,2,128,256]{3,2,1,0:T(8,128)}, f32[2,2,128,256]{3,2,1,0:T(8,128)S(1)}, u32[]{:S(2)}, u32[]{:S(2)}) collective-permute-start(f32[2,2,128,256]{3,2,1,0:T(8,128)} %get-tuple-element.16), channel_id=1, source_target_pairs={{0,1},{1,0},{2,3},{3,2},{4,5},{5,4},{6,7},{7,6},{8,9},{9,8},{10,11... | collective-permute-start | bytes 1572872 | tf_op jit(solution)/shard_map/ppermute | solution.py:190
  99.0 18.2 %all-to-all-start.3 = ((f32[128,8,128]{2,1,0:T(8,128)}), f32[128,8,128]{2,1,0:T(8,128)S(1)}, u32[]{:S(2)}, u32[]{:S(2)}) async-start(f32[128,8,128]{2,1,0:T(8,128)} %broadcast_in_dim.33), calls=%async_computation.3 | async-start | bytes 1048576 | tf_op jit(solution)/shard_map/all_to_all | solution.py:194
where the time goes:
time: 120 us; the launch traced here: 119 us
  waiting for transfers between devices  33.6 us (28%)
  blocking collectives  29.3 us (24%)
  starting transfers between devices  23.5 us (20%)
  Pallas kernels  15.7 us (13%)
  local copies, waits for them, and re-layouts  8.66 us (7%)
  matrix products  6.12 us (5%)
  between operations  2.04 us (2%)
    all_to_all x1, blocking collectives, per_device(): mine = lax.all_to_all(spread, 'basis', 0, 0, tiled=True)  29.3 us
    all_to_all x1, waiting for transfers between devices, per_device(): lax.all_to_all(jnp.broadcast_to(lam, parts.shape), both, 0, 0, tiled=True)  13.7 us
    all_to_all x1, waiting for transfers between devices, per_device(): parts = lax.all_to_all(squares, both, 0, 0, tiled=True)  12.6 us
    all_to_all x1, starting transfers between devices, per_device(): lax.all_to_all(slots.reshape(pairs * n_basis, ROWS, pw), ('ex', 'basis'),...  11.9 us
    all_to_all x1, waiting for transfers between devices, per_device(): lax.all_to_all(slots.reshape(pairs * n_basis, ROWS, pw), ('ex', 'basis'),...  7.28 us
    pallas_call x1, Pallas kernels, turned(): pl.pallas_call(turn_kernel, grid=(local,), in_specs=[pl.BlockSpec((1, wid...  6.98 us
    dot_general x1, matrix products, per_device(): lax.dot_general(grad_basis, out_grads, (((0,), (2,)), ((), ())), preferre...  6.12 us
    all_to_all x1, starting transfers between devices, per_device(): lax.all_to_all(jnp.broadcast_to(lam, parts.shape), both, 0, 0, tiled=True)  4.51 us
  transfers between devices with their start and end apart: 5, of which 3 were waited for; matrix products, arithmetic and copies ran while one was open for 6% of the time, Pallas kernels for 8%

commit v1 on v0

--- a/solution.py
+++ b/solution.py
@@ -1,3 +1,5 @@
+import functools
+
 import jax
 import jax.numpy as jnp
 from jax import lax
@@ -16,20 +18,58 @@
     return [pl.BlockSpec(memory_space=pltpu.VMEM)] * n
 
 
-def turn_kernel(x_ref, o_ref):
-    o_ref[0] = x_ref[0].T
+def lay_kernel(cuts, x_ref, o_ref, held, sems):
+    pairs, blocks = x_ref.shape[:2]
+    step = blocks // cuts
+    takes, gives = [], []
+    for p in range(pairs):
+        for i in range(cuts):
+            at = pl.ds(i * step, step)
+            k = p * cuts + i
+            takes.append(pltpu.make_async_copy(x_ref.at[p, at], held.at[p, at], sems.at[0, k]))
+            gives.append(pltpu.make_async_copy(held.at[p, at], o_ref.at[p, at], sems.at[1, k]))
+    for c in takes:
+        c.start()
+    for c, d in zip(takes, gives):
+        c.wait()
+        d.start()
+    for d in gives:
+        d.wait()
+
+
+def laid(slots, n_basis):
+    pairs, blocks, rows, width = slots.shape
+    cuts = 3
+    return pl.pallas_call(
+        functools.partial(lay_kernel, cuts),
+        in_specs=[pl.BlockSpec(memory_space=pl.ANY)],
+        out_specs=pl.BlockSpec(memory_space=pl.ANY),
+        out_shape=pltpu.HBM((pairs, n_basis, rows, width), slots.dtype),
+        scratch_shapes=[pltpu.VMEM(slots.shape, slots.dtype), pltpu.SemaphoreType.DMA((2, pairs * cuts))],
+        compiler_params=pltpu.CompilerParams(vmem_limit_bytes=4 << 20),
+    )(pltpu.with_memory_space_constraint(slots, pltpu.HBM))
+
+
+def turn_kernel(x_ref, *o_refs):
+    parts = x_ref.shape[2] // TT
+    for i, o_ref in enumerate(o_refs):
+
+        @pl.when(pl.program_id(0) == i // parts)
+        def _():
+            o_ref[...] = x_ref[0, :, pl.ds(i % parts * TT, TT)].T
 
 
 def turned(activations):
     local, tok, width = activations.shape
     x = pltpu.with_memory_space_constraint(jnp.swapaxes(activations, 1, 2), pltpu.HBM)
+    count = local * tok // TT
     return pl.pallas_call(
         turn_kernel,
         grid=(local,),
         in_specs=[pl.BlockSpec((1, width, tok), lambda n: (n, 0, 0))],
-        out_specs=pl.BlockSpec((1, tok, width), lambda n: (n, 0, 0)),
-        out_shape=pltpu.HBM((local, tok, width), BF16),
-        compiler_params=pltpu.CompilerParams(vmem_limit_bytes=28 << 20),
+        out_specs=[pl.BlockSpec((TT, width), lambda n: (0, 0))] * count,
+        out_shape=[pltpu.HBM((TT, width), BF16)] * count,
+        compiler_params=pltpu.CompilerParams(vmem_limit_bytes=40 << 20),
         cost_estimate=pl.CostEstimate(flops=0, transcendentals=0, bytes_accessed=4 * local * tok * width),
     )(x)
 
@@ -44,27 +84,31 @@
     return jnp.concatenate(cols, axis=1)
 
 
-def pair_products(act_ref, rg_ref, basis_ref, rot):
-    local, tok, _ = act_ref.shape
-    pair = pair_of_panels(basis_ref)
-    for n in range(local):
-        for t in range(0, tok, TT):
-            rows = pl.ds(t, TT)
-            rot[n, rows] = jnp.dot(act_ref[n, rows], pair, preferred_element_type=F32).astype(BF16)
-    return [jnp.dot(rg_ref[n], rot[n], preferred_element_type=F32) for n in range(local)]
-
-
-def first_kernel(act_ref, rg_ref, basis_ref, ex_ref, rot):
-    for n, ex in enumerate(pair_products(act_ref, rg_ref, basis_ref, rot)):
-        ex_ref[n] = ex
-
-
-def second_kernel(e_ref, act_ref, rg_ref, basis_ref, own_ref, keep_ref, send_ref, sq_ref, rot, ex_ref, sq):
+def rotate(act_refs, pair, rot, slot):
+    for t, act_ref in enumerate(act_refs):
+        rot[slot, pl.ds(t * TT, TT)] = jnp.dot(act_ref[...], pair, preferred_element_type=F32).astype(BF16)
+
+
+def first_kernel(*refs):
+    *act_refs, rg_ref, basis_ref, ex_ref, rot = refs
+    rotate(act_refs, pair_of_panels(basis_ref), rot, 0)
+    ex_ref[...] = jnp.dot(rg_ref[0], rot[0], preferred_element_type=F32)
+
+
+def second_kernel(e_ref, *refs):
+    *act_refs, rg_ref, mine_ref, other_ref, own0_ref, keep_ref, send_ref, sq_ref, rot, own_ref, ex_ref = refs
     e = e_ref[0]
     local, dirs, cols = own_ref.shape
     mid = dirs // 2
-    for n, ex in enumerate(pair_products(act_ref, rg_ref, basis_ref, rot)):
-        ex_ref[n] = ex
+    parts = len(act_refs) // local
+    rotate(act_refs[parts:], pair_of_panels(mine_ref), rot, 0)
+    pair = pair_of_panels(other_ref)
+    rotate(act_refs[:parts], pair, rot, 1)
+    rotate(act_refs[parts:], pair, rot, 2)
+    own_ref[0] = own0_ref[...]
+    own_ref[1] = jnp.dot(rg_ref[1], rot[0], preferred_element_type=F32)
+    for n in range(local):
+        ex_ref[n] = jnp.dot(rg_ref[n], rot[1 + n], preferred_element_type=F32)
     here, there = (pl.ds(pl.multiple_of(x * mid, 8), mid) for x in (e, 1 - e))
     for n in range(local):
         for side, src in enumerate((own_ref, ex_ref)):
@@ -83,23 +127,27 @@
 
 
 def ex_gradients(e, act, rg, mine, other):
-    local, tok, width = act.shape
-    dirs = rg.shape[1]
-    cost = pl.CostEstimate(
-        flops=2 * local * tok * width * 256, transcendentals=0, bytes_accessed=2 * local * tok * width
-    )
+    local, dirs, tok = rg.shape
+    width = act[0].shape[1]
+    parts = len(act) // local
+
+    def cost(count):
+        return pl.CostEstimate(
+            flops=2 * count * tok * width * 256, transcendentals=0, bytes_accessed=2 * count * tok * width
+        )
+
     own = pl.pallas_call(
         first_kernel,
-        in_specs=in_vmem(3),
+        in_specs=in_vmem(parts + 2),
         out_specs=pl.BlockSpec(memory_space=pltpu.VMEM),
-        out_shape=pltpu.VMEM((local, dirs, 256), F32),
-        scratch_shapes=[pltpu.VMEM((local, tok, 256), BF16)],
+        out_shape=pltpu.VMEM((dirs, 256), F32),
+        scratch_shapes=[pltpu.VMEM((1, tok, 256), BF16)],
         compiler_params=pltpu.CompilerParams(vmem_limit_bytes=16 << 20),
-        cost_estimate=cost,
-    )(act, rg, mine)
+        cost_estimate=cost(1),
+    )(*act[:parts], rg, mine)
     return pl.pallas_call(
         second_kernel,
-        in_specs=[pl.BlockSpec(memory_space=pltpu.SMEM)] + in_vmem(4),
+        in_specs=[pl.BlockSpec(memory_space=pltpu.SMEM)] + in_vmem(len(act) + 4),
         out_specs=in_vmem(3),
         out_shape=[
             pltpu.HBM((local, 2, dirs // 2, 256), F32),
@@ -107,13 +155,13 @@
             pltpu.HBM((dirs * 512 // 1024, 8, 128), F32),
         ],
         scratch_shapes=[
-            pltpu.VMEM((local, tok, 256), BF16),
+            pltpu.VMEM((3, tok, 256), BF16),
             pltpu.VMEM((local, dirs, 256), F32),
-            pltpu.VMEM((dirs, 256), F32),
+            pltpu.VMEM((local, dirs, 256), F32),
         ],
         compiler_params=pltpu.CompilerParams(vmem_limit_bytes=16 << 20),
-        cost_estimate=cost,
-    )(e, act, rg, other, own)
+        cost_estimate=cost(3),
+    )(e, *act, rg, mine, other, own)
 
 
 def scale_kernel(e_ref, lam_ref, keep_ref, got_ref, o_ref, inv):
@@ -169,8 +217,7 @@
     blocks = half // ROWS
     pairs = panels // 2
 
-    slots = panel_store.reshape(pairs, 2 * blocks, ROWS, pw)
-    slots = jnp.pad(slots, ((0, 0), (0, n_basis - 2 * blocks), (0, 0), (0, 0)))
+    slots = laid(panel_store.reshape(pairs, 2 * blocks, ROWS, pw), n_basis)
     arrived = lax.all_to_all(slots.reshape(pairs * n_basis, ROWS, pw), ("ex", "basis"), 0, 0, tiled=True)
     act = turned(activations)
     rg = lax.dot_general(grad_basis, out_grads, (((0,), (2,)), ((), ())), preferred_element_type=F32)

time: 120 us -> 118 us (0.983)
  local copies, waits for them, and re-layouts: 8.66 us -> 2.42 us
  Pallas kernels: 15.7 us -> 19.8 us
    unnamed x10 -> x20, local copies, waits for them, and re-layouts: 3.59 us -> 0.04 us
    pad x1 -> x0, local copies, waits for them, and re-layouts: 2.72 us -> none  [per_device(): slots = jnp.pad(slots, ((0, 0), (0, n_basis - 2 * blocks), (0, 0), (0, 0)))]
    pallas_call x1, Pallas kernels: 4.03 us -> 5.57 us  [ex_gradients(): pl.pallas_call(second_kernel, in_specs=[pl.BlockSpec(memory_space=pltpu.S...]
    ppermute x1, waiting for transfers between devices: 0.01 us -> 1.34 us  [per_device(): other = lax.ppermute(mine, 'ex', swap)]
    all_to_all x1, waiting for transfers between devices: 7.28 us -> 5.96 us  [per_device(): lax.all_to_all(slots.reshape(pairs * n_basis, ROWS, pw), ('ex', 'basis'),...]
    pallas_call x1, Pallas kernels: 6.98 us -> 8.29 us  [turned(): pl.pallas_call(turn_kernel, grid=(local,), in_specs=[pl.BlockSpec((1, wid...]
    pallas_call x1 -> x2, Pallas kernels: 2.84 us -> 4.07 us  [the longest x1 2.39 us: laid(): pl.pallas_call(functools.partial(lay_kernel, cuts), in_specs=[pl.BlockSpe...]
  transfers between devices with their start and end apart: 5 -> 5, of which waited for: 3 -> 4; matrix products, arithmetic and copies ran while one was open for 6% -> 7% of each run, Pallas kernels for 8% -> 8%
where the time goes in v1:
time: 118 us
  waiting for transfers between devices  33.6 us (28%)
  blocking collectives  29.5 us (25%)
  starting transfers between devices  23.8 us (20%)
  Pallas kernels  19.8 us (17%)
  matrix products  6.12 us (5%)
  local copies, waits for them, and re-layouts  2.42 us (2%)
  between operations  2.08 us (2%)
    all_to_all x1, blocking collectives, per_device(): mine = lax.all_to_all(spread, 'basis', 0, 0, tiled=True)  29.5 us
    all_to_all x1, waiting for transfers between devices, per_device(): lax.all_to_all(jnp.broadcast_to(lam, parts.shape), both, 0, 0, tiled=True)  13.7 us
    all_to_all x1, waiting for transfers between devices, per_device(): parts = lax.all_to_all(squares, both, 0, 0, tiled=True)  12.6 us
    all_to_all x1, starting transfers between devices, per_device(): lax.all_to_all(slots.reshape(pairs * n_basis, ROWS, pw), ('ex', 'basis'),...  11.9 us
    pallas_call x1, Pallas kernels, turned(): pl.pallas_call(turn_kernel, grid=(local,), in_specs=[pl.BlockSpec((1, wid...  8.29 us
    dot_general x1, matrix products, per_device(): lax.dot_general(grad_basis, out_grads, (((0,), (2,)), ((), ())), preferre...  6.12 us
    all_to_all x1, waiting for transfers between devices, per_device(): lax.all_to_all(slots.reshape(pairs * n_basis, ROWS, pw), ('ex', 'basis'),...  5.96 us
    pallas_call x1, Pallas kernels, ex_gradients(): pl.pallas_call(second_kernel, in_specs=[pl.BlockSpec(memory_space=pltpu.S...  5.57 us
  transfers between devices with their start and end apart: 5, of which 4 were waited for; matrix products, arithmetic and copies ran while one was open for 7% of the time, Pallas kernels for 8%

profile of v1, /device:TPU:1, one launch (start us, length us, event | category | flops | bytes accessed | tf_op | source)
XLA Modules:
  0.0 117.6 jit_solution(2589382805824980401)
XLA Ops:
  0.0 0.0 copy-start
  0.0 2.4 %shard_map.64 = bf16[2,64,48,128]{3,2,1,0:T(8,128)(2,1)} custom-call(bf16[2,60,48,128]{3,2,1,0:T(8,128)(2,1)} %bitcast.24), custom_call_target="tpu_custom_call" | custom-call | tf_op jit(solution)/shard_map/pallas_call | solution.py:43
  2.4 0.0 copy-start.9
  2.4 11.9 %all-to-all-start = ((bf16[128,48,128]{2,1,0:T(8,128)(2,1)}), bf16[128,48,128]{2,1,0:T(8,128)(2,1)}, u32[]{:S(2)}, u32[]{:S(2)}) async-start(bf16[128,48,128]{2,1,0:T(8,128)(2,1)} %bitcast.23), calls=%async_computation | async-start | bytes 3145728 | tf_op jit(solution)/shard_map/all_to_all | solution.py:221
  14.3 0.0 copy-done.9
  14.3 0.6 dynamic_slice.7
  16.2 0.0 copy-start.8
  16.2 8.3 %shard_map.65 = (bf16[256,2880]{1,0:T(8,128)(2,1)}, bf16[256,2880]{1,0:T(8,128)(2,1)}, bf16[256,2880]{1,0:T(8,128)(2,1)}, bf16[256,2880]{1,0:T(8,128)(2,1)}, bf1...) custom-call(bf16[2,2880,768]{2,1,0:T(8,128)(2,1)} %bitcast.22), custom_call_target="tpu_custom_call" | custom-call | bytes 17694720 | tf_op jit(solution)/shard_map/pallas_call | solution.py:66
  25.2 0.0 copy-done.8
  25.2 0.1 iota_compare_fusion
  25.3 0.0 copy-done
  25.3 6.1 %fusion.8.refs_3_.refs_6_ = bf16[2,256,768]{2,1,0:T(8,128)(2,1)S(1)} fusion(bf16[2,768,2880]{1,2,0:T(8,128)(2,1)} %param.7, bf16[2880,256]{1,0:T(8,128)(2,1)S(1)} %copy-done, pred[2,768]{1,0:T(4,128)(4,1)S(1)} %iota_compare_fusion), kind=kOutput, calls=%fused_computation.4 | convolution fusion | flops 2265710592 | bytes 11109888 | tf_op jit(solution)/shard_map/dot_general | solution.py:223
  31.4 6.0 %all-to-all-done = bf16[128,48,128]{2,1,0:T(8,128)(2,1)} async-done(((bf16[128,48,128]{2,1,0:T(8,128)(2,1)}), bf16[128,48,128]{2,1,0:T(8,128)(2,1)}, u32[]{:S(2)}, u32[]{:S(2)}) %all-to-all-start) | async-done | bytes 1572896 | tf_op jit(solution)/shard_map/all_to_all | solution.py:221
  37.4 0.7 dynamic-slice_bitcast_fusion
  38.1 0.2 broadcast_in_dim.32
  38.3 0.0 copy-start.1
  38.3 0.0 copy-start.2
  38.3 29.5 %all_to_all.20.refs_4_.refs_7_ = bf16[64,2,48,128]{3,2,1,0:T(8,128)(2,1)S(1)} all-to-all(bf16[64,2,48,128]{3,2,1,0:T(8,128)(2,1)S(1)} %broadcast_in_dim.32), channel_id=1, replica_groups=mesh['basis'=64,'ex'=2] {'basis'}, dimensions={0} | all-to-all | bytes 3145728 | tf_op jit(solution)/shard_map/all_to_all | solution.py:232
  67.9 2.1 %collective-permute-start = (bf16[64,2,48,128]{3,2,1,0:T(8,128)(2,1)S(1)}, bf16[64,2,48,128]{3,2,1,0:T(8,128)(2,1)S(1)}, u32[]{:S(2)}, u32[]{:S(2)}) collective-permute-start(bf16[64,2,48,128]{3,2,1,0:T(8,128)(2,1)S(1)} %all_to_all.20.refs_4_.refs_7_), channel_id=1, source_target_pairs={{0,1},{1,0},{2,3},{3,2},{4,5},{5,4},{6,7},{7,6},{8,9},{9,8},{10,11... | collective-permute-start | bytes 4718600 | tf_op jit(solution)/shard_map/ppermute | solution.py:235
  70.0 1.7 %shard_map.66.refs_9_ = f32[256,256]{1,0:T(8,128)S(1)} custom-call(bf16[256,2880]{1,0:T(8,128)(2,1)S(1)} %copy-done.1, bf16[256,2880]{1,0:T(8,128)(2,1)S(1)} %copy-done.2, bf16[256,2880]{1,0:T(8,128)(2,1)S(1)} %copy-done.3, bf16[2,256,768]{2,1,0:T(8,128)(2,1)S(1)} %fusion.8.refs_3_.refs_6_, bf16[64,2,48,128]{3,2,1,0:T(8,128)(2,1)S(1)} %all_to_all.20.refs_4_.refs_7_), custom_call_target="tpu_custom_call" | custom-call | flops 1132462080 | bytes 4423680 | tf_op jit(solution)/shard_map/pallas_call | solution.py:139
  71.7 1.3 %collective-permute-done.refs_8_ = bf16[64,2,48,128]{3,2,1,0:T(8,128)(2,1)S(1)} collective-permute-done((bf16[64,2,48,128]{3,2,1,0:T(8,128)(2,1)S(1)}, bf16[64,2,48,128]{3,2,1,0:T(8,128)(2,1)S(1)}, u32[]{:S(2)}, u32[]{:S(2)}) %collective-permute-start) | collective-permute-done | bytes 1572896 | tf_op jit(solution)/shard_map/ppermute | solution.py:235
  73.0 5.6 %shard_map.67 = (f32[2,2,128,256]{3,2,1,0:T(8,128)}, f32[2,2,128,256]{3,2,1,0:T(8,128)}, f32[128,8,128]{2,1,0:T(8,128)}) custom-call(s32[1]{0:T(128)} %bitcast.e_ref, bf16[256,2880]{1,0:T(8,128)(2,1)S(1)} %copy-done.1, bf16[256,2880]{1,0:T(8,128)(2,1)S(1)} %copy-done.2, bf16[256,2880]{1,0:T(8,128)(2,1)S(1)} %copy-done.3, bf16[256,2880]{1,0:T(8,128)(2,1)S(1)} %copy-done.4, ...), custom_call_target="tpu_custom_call" | custom-call | flops 3397386240 | bytes 13271040 | tf_op jit(solution)/shard_map/pallas_call | solution.py:148
  78.6 4.2 %all-to-all-start.2 = ((f32[128,8,128]{2,1,0:T(8,128)}), f32[128,8,128]{2,1,0:T(8,128)S(1)}, u32[]{:S(2)}, u32[]{:S(2)}) async-start(f32[128,8,128]{2,1,0:T(8,128)} %get-tuple-element.36), calls=%async_computation.2 | async-start | bytes 1048576 | tf_op jit(solution)/shard_map/all_to_all | solution.py:239
  82.8 1.1 collective-permute-start.1
  83.9 12.6 %all-to-all-done.2 = f32[128,8,128]{2,1,0:T(8,128)S(1)} async-done(((f32[128,8,128]{2,1,0:T(8,128)}), f32[128,8,128]{2,1,0:T(8,128)S(1)}, u32[]{:S(2)}, u32[]{:S(2)}) %all-to-all-start.2) | async-done | bytes 524320 | tf_op jit(solution)/shard_map/all_to_all | solution.py:239
  96.5 0.1 reduce_sum.9
  96.6 0.8 broadcast_in_dim.33
  97.5 4.5 %all-to-all-start.3 = ((f32[128,8,128]{2,1,0:T(8,128)}), f32[128,8,128]{2,1,0:T(8,128)S(1)}, u32[]{:S(2)}, u32[]{:S(2)}) async-start(f32[128,8,128]{2,1,0:T(8,128)} %broadcast_in_dim.33), calls=%async_computation.3 | async-start | bytes 1048576 | tf_op jit(solution)/shard_map/all_to_all | solution.py:241
  102.0 0.0 collective-permute-done.1.got_ref
  102.0 13.7 %all-to-all-done.3.lam_ref = f32[128,8,128]{2,1,0:T(8,128)S(1)} async-done(((f32[128,8,128]{2,1,0:T(8,128)}), f32[128,8,128]{2,1,0:T(8,128)S(1)}, u32[]{:S(2)}, u32[]{:S(2)}) %all-to-all-start.3) | async-done | bytes 524320 | tf_op jit(solution)/shard_map/all_to_all | solution.py:241
  115.7 0.0 copy-done.7
  115.7 1.9 %shard_map.68 = f32[4,128,512]{2,1,0:T(8,128)} custom-call(s32[1]{0:T(128)} %bitcast.e_ref, f32[128,8,128]{2,1,0:T(8,128)S(1)} %all-to-all-done.3.lam_ref, f32[2,2,128,256]{3,2,1,0:T(8,128)S(1)} %copy-done.7, f32[2,2,128,256]{3,2,1,0:T(8,128)S(1)} %collective-permute-done.1.got_ref), custom_call_target="tpu_custom_call" | custom-call | tf_op jit(solution)/shard_map/pallas_call | solution.py:197
  (12 shorter events, 0.0 us)
Async XLA Ops:
  0.0 25.3 %copy-start = (bf16[2880,256]{1,0:T(8,128)(2,1)S(1)}, bf16[2880,256]{1,0:T(8,128)(2,1)}, u32[]{:S(2)}) copy-start(bf16[2880,256]{1,0:T(8,128)(2,1)} %param.8) | copy-start | bytes 4423684
  2.4 11.9 %copy-start.9 = (s32[4]{0:T(128)S(1)}, s32[4]{0:T(128)}, u32[]{:S(2)}) copy-start(s32[4]{0:T(128)} %param.10) | copy-start | bytes 52
  2.4 35.0 %all-to-all-start = ((bf16[128,48,128]{2,1,0:T(8,128)(2,1)}), bf16[128,48,128]{2,1,0:T(8,128)(2,1)}, u32[]{:S(2)}, u32[]{:S(2)}) async-start(bf16[128,48,128]{2,1,0:T(8,128)(2,1)} %bitcast.23), calls=%async_computation | async-start | bytes 3145728 | tf_op jit(solution)/shard_map/all_to_all | solution.py:221
  16.2 9.0 %copy-start.8 = (s32[2]{0:T(128)S(1)}, s32[2]{0:T(128)}, u32[]{:S(2)}) copy-start(s32[2]{0:T(128)} %param.11) | copy-start | bytes 28
  38.1 31.9 %copy-start.3 = (bf16[256,2880]{1,0:T(8,128)(2,1)S(1)}, bf16[256,2880]{1,0:T(8,128)(2,1)}, u32[]{:S(2)}) copy-start(bf16[256,2880]{1,0:T(8,128)(2,1)} %get-tuple-element.30.refs_2_) | copy-start | bytes 4423684
  38.3 31.7 %copy-start.1 = (bf16[256,2880]{1,0:T(8,128)(2,1)S(1)}, bf16[256,2880]{1,0:T(8,128)(2,1)}, u32[]{:S(2)}) copy-start(bf16[256,2880]{1,0:T(8,128)(2,1)} %get-tuple-element.28.refs_0_) | copy-start | bytes 4423684
  38.3 31.7 %copy-start.2 = (bf16[256,2880]{1,0:T(8,128)(2,1)S(1)}, bf16[256,2880]{1,0:T(8,128)(2,1)}, u32[]{:S(2)}) copy-start(bf16[256,2880]{1,0:T(8,128)(2,1)} %get-tuple-element.29.refs_1_) | copy-start | bytes 4423684
  67.9 5.1 %copy-start.4 = (bf16[256,2880]{1,0:T(8,128)(2,1)S(1)}, bf16[256,2880]{1,0:T(8,128)(2,1)}, u32[]{:S(2)}) copy-start(bf16[256,2880]{1,0:T(8,128)(2,1)} %get-tuple-element.31.refs_3_) | copy-start | bytes 4423684
  67.9 5.1 %copy-start.5 = (bf16[256,2880]{1,0:T(8,128)(2,1)S(1)}, bf16[256,2880]{1,0:T(8,128)(2,1)}, u32[]{:S(2)}) copy-start(bf16[256,2880]{1,0:T(8,128)(2,1)} %get-tuple-element.32.refs_4_) | copy-start | bytes 4423684
  67.9 5.1 %copy-start.6 = (bf16[256,2880]{1,0:T(8,128)(2,1)S(1)}, bf16[256,2880]{1,0:T(8,128)(2,1)}, u32[]{:S(2)}) copy-start(bf16[256,2880]{1,0:T(8,128)(2,1)} %get-tuple-element.33.refs_5_) | copy-start | bytes 4423684
  67.9 5.1 %collective-permute-start = (bf16[64,2,48,128]{3,2,1,0:T(8,128)(2,1)S(1)}, bf16[64,2,48,128]{3,2,1,0:T(8,128)(2,1)S(1)}, u32[]{:S(2)}, u32[]{:S(2)}) collective-permute-start(bf16[64,2,48,128]{3,2,1,0:T(8,128)(2,1)S(1)} %all_to_all.20.refs_4_.refs_7_), channel_id=1, source_target_pairs={{0,1},{1,0},{2,3},{3,2},{4,5},{5,4},{6,7},{7,6},{8,9},{9,8},{10,11... | collective-permute-start | bytes 4718600 | tf_op jit(solution)/shard_map/ppermute | solution.py:235
  78.6 37.1 %copy-start.7 = (f32[2,2,128,256]{3,2,1,0:T(8,128)S(1)}, f32[2,2,128,256]{3,2,1,0:T(8,128)}, u32[]{:S(2)}) copy-start(f32[2,2,128,256]{3,2,1,0:T(8,128)} %get-tuple-element.37.keep_ref) | copy-start | bytes 1572868
  78.6 17.9 %all-to-all-start.2 = ((f32[128,8,128]{2,1,0:T(8,128)}), f32[128,8,128]{2,1,0:T(8,128)S(1)}, u32[]{:S(2)}, u32[]{:S(2)}) async-start(f32[128,8,128]{2,1,0:T(8,128)} %get-tuple-element.36), calls=%async_computation.2 | async-start | bytes 1048576 | tf_op jit(solution)/shard_map/all_to_all | solution.py:239
  82.8 19.2 %collective-permute-start.1 = (f32[2,2,128,256]{3,2,1,0:T(8,128)}, f32[2,2,128,256]{3,2,1,0:T(8,128)S(1)}, u32[]{:S(2)}, u32[]{:S(2)}) collective-permute-start(f32[2,2,128,256]{3,2,1,0:T(8,128)} %get-tuple-element.38), channel_id=1, source_target_pairs={{0,1},{1,0},{2,3},{3,2},{4,5},{5,4},{6,7},{7,6},{8,9},{9,8},{10,11... | collective-permute-start | bytes 1572872 | tf_op jit(solution)/shard_map/ppermute | solution.py:237
  97.5 18.2 %all-to-all-start.3 = ((f32[128,8,128]{2,1,0:T(8,128)}), f32[128,8,128]{2,1,0:T(8,128)S(1)}, u32[]{:S(2)}, u32[]{:S(2)}) async-start(f32[128,8,128]{2,1,0:T(8,128)} %broadcast_in_dim.33), calls=%async_computation.3 | async-start | bytes 1048576 | tf_op jit(solution)/shard_map/all_to_all | solution.py:241

commit v2 on v1

--- a/solution.py
+++ b/solution.py
@@ -7,9 +7,9 @@
 from jax.experimental.pallas import tpu as pltpu
 from jax.sharding import PartitionSpec as P
 
-ROWS = 48
+ROWS = 24
 TT = 256
-HALF = 1440
+GT = 768
 F32 = jnp.float32
 BF16 = jnp.bfloat16
 
@@ -18,18 +18,23 @@
     return [pl.BlockSpec(memory_space=pltpu.VMEM)] * n
 
 
-def lay_kernel(cuts, x_ref, o_ref, held, sems):
-    pairs, blocks = x_ref.shape[:2]
+def lay_kernel(cuts, owners_ref, x_ref, o_ref, shared_ref, held, sems):
+    pairs, blocks = held.shape[:2]
     step = blocks // cuts
+    me = lax.axis_index("basis")
     takes, gives = [], []
     for p in range(pairs):
+        second = (owners_ref[2 * p] != me) & (owners_ref[2 * p + 1] == me)
+        panel = 2 * p + jnp.where(second, 1, 0)
         for i in range(cuts):
             at = pl.ds(i * step, step)
             k = p * cuts + i
-            takes.append(pltpu.make_async_copy(x_ref.at[p, at], held.at[p, at], sems.at[0, k]))
+            takes.append(pltpu.make_async_copy(x_ref.at[panel, at], held.at[p, at], sems.at[0, k]))
             gives.append(pltpu.make_async_copy(held.at[p, at], o_ref.at[p, at], sems.at[1, k]))
     for c in takes:
         c.start()
+    shared = [jnp.where(owners_ref[2 * p] == owners_ref[2 * p + 1], 1, 0) for p in range(pairs)]
+    shared_ref[0] = sum(shared)
     for c, d in zip(takes, gives):
         c.wait()
         d.start()
@@ -37,17 +42,99 @@
         d.wait()
 
 
-def laid(slots, n_basis):
-    pairs, blocks, rows, width = slots.shape
-    cuts = 3
+def laid(owners, slots, n_basis):
+    panels, blocks, rows, width = slots.shape
+    pairs, cuts = panels // 2, 3
     return pl.pallas_call(
         functools.partial(lay_kernel, cuts),
-        in_specs=[pl.BlockSpec(memory_space=pl.ANY)],
-        out_specs=pl.BlockSpec(memory_space=pl.ANY),
-        out_shape=pltpu.HBM((pairs, n_basis, rows, width), slots.dtype),
-        scratch_shapes=[pltpu.VMEM(slots.shape, slots.dtype), pltpu.SemaphoreType.DMA((2, pairs * cuts))],
+        in_specs=[pl.BlockSpec(memory_space=pltpu.SMEM), pl.BlockSpec(memory_space=pl.ANY)],
+        out_specs=[pl.BlockSpec(memory_space=pl.ANY), pl.BlockSpec(memory_space=pltpu.SMEM)],
+        out_shape=[
+            pltpu.HBM((pairs, n_basis, rows, width), slots.dtype),
+            jax.ShapeDtypeStruct((1,), jnp.int32),
+        ],
+        scratch_shapes=[
+            pltpu.VMEM((pairs, blocks, rows, width), slots.dtype),
+            pltpu.SemaphoreType.DMA((2, pairs * cuts)),
+        ],
         compiler_params=pltpu.CompilerParams(vmem_limit_bytes=4 << 20),
-    )(pltpu.with_memory_space_constraint(slots, pltpu.HBM))
+    )(owners, pltpu.with_memory_space_constraint(slots, pltpu.HBM))
+
+
+def pick_kernel(owners_ref, x_ref, second_ref, o_ref, block, sems):
+    rows = x_ref.shape[2]
+    first = 2 * lax.axis_index("ex")
+    owner0, owner1 = owners_ref[first], owners_ref[first + 1]
+
+    def fetches(second):
+        src = second_ref if second else x_ref.at[:, owner1]
+        out = []
+        for h in range(2):
+            at = pl.ds(h * rows, rows)
+            out.append(pltpu.make_async_copy(x_ref.at[h, owner0], block.at[0, at], sems.at[h]))
+            out.append(pltpu.make_async_copy(src.at[h], block.at[1, at], sems.at[2 + h]))
+        return out
+
+    for second in range(2):
+
+        @pl.when((owner0 == owner1) == bool(second))
+        def _():
+            for c in fetches(second):
+                c.start()
+            for c in fetches(second):
+                c.wait()
+
+    for j in range(o_ref.shape[0]):
+        o_ref[j] = block[...]
+
+
+def picked(owners, arrived, second):
+    _, n_basis, rows, width = arrived.shape
+    return pl.pallas_call(
+        pick_kernel,
+        in_specs=[pl.BlockSpec(memory_space=pltpu.SMEM)] + [pl.BlockSpec(memory_space=pl.ANY)] * 2,
+        out_specs=pl.BlockSpec(memory_space=pltpu.VMEM),
+        out_shape=pltpu.VMEM((n_basis, 2, 2 * rows, width), arrived.dtype),
+        scratch_shapes=[pltpu.VMEM((2, 2 * rows, width), arrived.dtype), pltpu.SemaphoreType.DMA((4,))],
+        compiler_params=pltpu.CompilerParams(vmem_limit_bytes=1 << 20),
+    )(owners, arrived, second)
+
+
+def rot_grad_kernel(count_ref, basis_ref, x_ref, o_ref, turned_basis):
+    n, t = pl.program_id(0), pl.program_id(1)
+    step = o_ref.shape[2]
+
+    @pl.when((n == 0) & (t == 0))
+    def _():
+        turned_basis[...] = basis_ref[...].T
+
+    rot = jnp.dot(turned_basis[...], x_ref[0], preferred_element_type=F32).astype(BF16)
+    live = t * step + lax.broadcasted_iota(jnp.int32, rot.shape, 1) < count_ref[n]
+    o_ref[0] = jnp.where(live, rot, jnp.zeros_like(rot))
+
+
+def rotated_grads(token_count, grad_basis, out_grads):
+    local, tok, width = out_grads.shape
+    dirs = grad_basis.shape[1]
+    x = pltpu.with_memory_space_constraint(jnp.swapaxes(out_grads, 1, 2), pltpu.HBM)
+    return pl.pallas_call(
+        rot_grad_kernel,
+        grid_spec=pltpu.PrefetchScalarGridSpec(
+            num_scalar_prefetch=1,
+            grid=(local, tok // GT),
+            in_specs=[
+                pl.BlockSpec((width, dirs), lambda n, t, count: (0, 0)),
+                pl.BlockSpec((1, width, GT), lambda n, t, count: (n, 0, t)),
+            ],
+            out_specs=pl.BlockSpec((1, dirs, GT), lambda n, t, count: (n, 0, t)),
+            scratch_shapes=[pltpu.VMEM((dirs, width), BF16)],
+        ),
+        out_shape=jax.ShapeDtypeStruct((local, dirs, tok), BF16),
+        compiler_params=pltpu.CompilerParams(vmem_limit_bytes=28 << 20),
+        cost_estimate=pl.CostEstimate(
+            flops=2 * local * tok * width * dirs, transcendentals=0, bytes_accessed=2 * local * tok * width
+        ),
+    )(token_count, grad_basis, x)
 
 
 def turn_kernel(x_ref, *o_refs):
@@ -56,7 +143,8 @@
 
         @pl.when(pl.program_id(0) == i // parts)
         def _():
-            o_ref[...] = x_ref[0, :, pl.ds(i % parts * TT, TT)].T
+            x = x_ref[0, :, pl.ds(i % parts * TT, TT)].reshape(2, -1, ROWS, TT)
+            o_ref[...] = jnp.swapaxes(x, 0, 1).reshape(-1, TT).T
 
 
 def turned(activations):
@@ -74,14 +162,9 @@
     )(x)
 
 
-def pair_of_panels(ref):
-    half = HALF
-    blocks = half // ROWS
-    cols = []
-    for k in range(2):
-        rows = [ref[pl.ds(k * blocks, blocks), h].reshape(half, 128) for h in range(2)]
-        cols.append(jnp.concatenate(rows, axis=0))
-    return jnp.concatenate(cols, axis=1)
+def pair_of_panels(ref, width):
+    senders = width // ref.shape[2]
+    return jnp.concatenate([ref[pl.ds(0, senders), k].reshape(width, 128) for k in range(2)], axis=1)
 
 
 def rotate(act_refs, pair, rot, slot):
@@ -91,18 +174,18 @@
 
 def first_kernel(*refs):
     *act_refs, rg_ref, basis_ref, ex_ref, rot = refs
-    rotate(act_refs, pair_of_panels(basis_ref), rot, 0)
+    rotate(act_refs, pair_of_panels(basis_ref, act_refs[0].shape[1]), rot, 0)
     ex_ref[...] = jnp.dot(rg_ref[0], rot[0], preferred_element_type=F32)
 
 
-def second_kernel(e_ref, *refs):
+def second_kernel(*refs):
     *act_refs, rg_ref, mine_ref, other_ref, own0_ref, keep_ref, send_ref, sq_ref, rot, own_ref, ex_ref = refs
-    e = e_ref[0]
+    e = lax.axis_index("ex")
     local, dirs, cols = own_ref.shape
     mid = dirs // 2
-    parts = len(act_refs) // local
-    rotate(act_refs[parts:], pair_of_panels(mine_ref), rot, 0)
-    pair = pair_of_panels(other_ref)
+    parts, width = len(act_refs) // local, act_refs[0].shape[1]
+    rotate(act_refs[parts:], pair_of_panels(mine_ref, width), rot, 0)
+    pair = pair_of_panels(other_ref, width)
     rotate(act_refs[:parts], pair, rot, 1)
     rotate(act_refs[parts:], pair, rot, 2)
     own_ref[0] = own0_ref[...]
@@ -126,7 +209,7 @@
                     sq_ref[2 * (2 * (cols // 128) * r + (cols // 128) * pair + c) + h] = tile
 
 
-def ex_gradients(e, act, rg, mine, other):
+def ex_gradients(act, rg, mine, other):
     local, dirs, tok = rg.shape
     width = act[0].shape[1]
     parts = len(act) // local
@@ -147,7 +230,7 @@
     )(*act[:parts], rg, mine)
     return pl.pallas_call(
         second_kernel,
-        in_specs=[pl.BlockSpec(memory_space=pltpu.SMEM)] + in_vmem(len(act) + 4),
+        in_specs=in_vmem(len(act) + 4),
         out_specs=in_vmem(3),
         out_shape=[
             pltpu.HBM((local, 2, dirs // 2, 256), F32),
@@ -161,11 +244,11 @@
         ],
         compiler_params=pltpu.CompilerParams(vmem_limit_bytes=16 << 20),
         cost_estimate=cost(3),
-    )(e, *act, rg, mine, other, own)
-
-
-def scale_kernel(e_ref, lam_ref, keep_ref, got_ref, o_ref, inv):
-    e, i = e_ref[0], pl.program_id(0)
+    )(*act, rg, mine, other, own)
+
+
+def scale_kernel(lam_ref, keep_ref, got_ref, o_ref, inv):
+    e, i = lax.axis_index("ex"), pl.program_id(0)
     local = keep_ref.shape[0]
     tiles, across = lam_ref.shape[0] // 2, 4
 
@@ -188,58 +271,60 @@
                         o_ref[0, :, at] = src[j, side] * inv[:, at]
 
 
-def scaled_rows(e, lam, keep, got):
+def scaled_rows(lam, keep, got):
     local, _, dirs, _ = keep.shape
 
     def whole(x):
-        return pl.BlockSpec(x.shape, lambda i, e: (0,) * x.ndim)
+        return pl.BlockSpec(x.shape, lambda i: (0,) * x.ndim)
 
     return pl.pallas_call(
         scale_kernel,
-        grid_spec=pltpu.PrefetchScalarGridSpec(
-            num_scalar_prefetch=1,
-            grid=(2 * local,),
-            in_specs=[whole(lam), whole(keep), whole(got)],
-            out_specs=pl.BlockSpec((1, dirs, 512), lambda i, e: (i, 0, 0)),
-            scratch_shapes=[pltpu.VMEM((dirs, 512), F32)],
-        ),
+        grid=(2 * local,),
+        in_specs=[whole(lam), whole(keep), whole(got)],
+        out_specs=pl.BlockSpec((1, dirs, 512), lambda i: (i, 0, 0)),
+        scratch_shapes=[pltpu.VMEM((dirs, 512), F32)],
         out_shape=jax.ShapeDtypeStruct((2 * local, dirs, 512), F32),
         compiler_params=pltpu.CompilerParams(vmem_limit_bytes=8 << 20),
-    )(e, lam, keep, got)
+    )(lam, keep, got)
 
 
 def per_device(activations, out_grads, grad_basis, panel_store, owners, token_count):
     local, tok, width = activations.shape
     _, panels, half, pw = panel_store.shape
     n_basis, n_ex = lax.axis_size("basis"), lax.axis_size("ex")
-    b, e = lax.axis_index("basis"), lax.axis_index("ex")
-    e1 = e.reshape(1).astype(jnp.int32)
     blocks = half // ROWS
-    pairs = panels // 2
-
-    slots = laid(panel_store.reshape(pairs, 2 * blocks, ROWS, pw), n_basis)
-    arrived = lax.all_to_all(slots.reshape(pairs * n_basis, ROWS, pw), ("ex", "basis"), 0, 0, tiled=True)
+
+    slots = panel_store.reshape(panels, blocks, ROWS, pw)
+    sent, shared = laid(owners, slots, n_basis)
+
+    def to_chips(x):
+        got = lax.all_to_all(x.reshape(-1, ROWS, pw), ("ex", "basis"), 0, 0, tiled=True)
+        return got.reshape(2, n_basis, ROWS, pw)
+
+    arrived = to_chips(sent)
     act = turned(activations)
-    rg = lax.dot_general(grad_basis, out_grads, (((0,), (2,)), ((), ())), preferred_element_type=F32)
-    rg = jnp.transpose(rg, (1, 0, 2)).astype(BF16)
-    live = jnp.arange(tok)[None, :] < token_count[:, None]
-    rg = jnp.where(live[:, None, :], rg, jnp.zeros((), BF16))
-    arrived, act, rg = lax.optimization_barrier((arrived, act, rg))
-
-    owner = owners[2 * e + jnp.where(b < blocks, 0, 1)]
-    block = lax.dynamic_index_in_dim(arrived.reshape(2, n_basis, ROWS, pw), owner, 1, keepdims=False)
-    spread = jnp.broadcast_to(block[None], (n_basis, 2, ROWS, pw))
-    mine = lax.all_to_all(spread, "basis", 0, 0, tiled=True)
+    rg = rotated_grads(token_count, grad_basis, out_grads)
+    arrived, slots, act, rg = lax.optimization_barrier((arrived, slots, act, rg))
+
+    def second_panels(slots):
+        second = to_chips(jnp.pad(slots[1::2], ((0, 0), (0, n_basis - blocks), (0, 0), (0, 0))))
+        owner = owners[2 * lax.axis_index("ex") + 1]
+        return lax.dynamic_index_in_dim(second, owner, 1, keepdims=False)
+
+    second = lax.cond(
+        shared[0] > 0, second_panels, lambda slots: jnp.zeros((2, ROWS, pw), slots.dtype), slots
+    )
+    mine = lax.all_to_all(picked(owners, arrived, second), "basis", 0, 0, tiled=True)
 
     swap = [(0, 1), (1, 0)]
     other = lax.ppermute(mine, "ex", swap)
-    keep, send, squares = ex_gradients(e1, act, rg, mine, other)
+    keep, send, squares = ex_gradients(act, rg, mine, other)
     got = lax.ppermute(send, "ex", swap)
     both = ("basis", "ex")
     parts = lax.all_to_all(squares, both, 0, 0, tiled=True)
     lam = jnp.sum(parts, axis=0, keepdims=True) * (1.0 / (local * n_basis * n_ex))
     lam = lax.all_to_all(jnp.broadcast_to(lam, parts.shape), both, 0, 0, tiled=True)
-    return scaled_rows(e1, lam, keep, got)
+    return scaled_rows(lam, keep, got)
 
 
 def solution(mesh):

time: 118 us -> 115 us (0.975)
  Pallas kernels: 19.8 us -> 27.7 us
  matrix products: 6.12 us -> 0 us
  waiting for transfers between devices: 33.6 us -> 28.5 us
  blocking collectives: 29.5 us -> 33.3 us
  local copies, waits for them, and re-layouts: 2.42 us -> 0.88 us
  between operations: 2.08 us -> 0.76 us
    pallas_call x2 -> x4, Pallas kernels: 7.46 us -> 14.5 us  [the longest x1 6.05 us: rotated_grads(): pl.pallas_call(rot_grad_kernel, grid_spec=pltpu.PrefetchScalarGridSpec(nu...]
    dot_general x1 -> x0, matrix products: 6.12 us -> none  [per_device(): lax.dot_general(grad_basis, out_grads, (((0,), (2,)), ((), ())), preferre...]
    all_to_all x1, waiting for transfers between devices: 5.96 us -> 0.87 us  [to_chips(): lax.all_to_all(x.reshape(-1, ROWS, pw), ('ex', 'basis'), 0, 0, tiled=True)]
    all_to_all x1, blocking collectives: 29.5 us -> 33.3 us  [per_device(): lax.all_to_all(picked(owners, arrived, second), 'basis', 0, 0, tiled=True)]
  transfers between devices with their start and end apart: 5 -> 5, of which waited for: 4 -> 4; matrix products, arithmetic and copies ran while one was open for 7% -> 1% of each run, Pallas kernels for 8% -> 14%
where the time goes in v2:
time: 115 us
  blocking collectives  33.3 us (29%)
  waiting for transfers between devices  28.5 us (25%)
  Pallas kernels  27.7 us (24%)
  starting transfers between devices  23.2 us (20%)
    all_to_all x1, blocking collectives, per_device(): lax.all_to_all(picked(owners, arrived, second), 'basis', 0, 0, tiled=True)  33.3 us
    all_to_all x1, waiting for transfers between devices, per_device(): lax.all_to_all(jnp.broadcast_to(lam, parts.shape), both, 0, 0, tiled=True)  13.7 us
    all_to_all x1, waiting for transfers between devices, per_device(): parts = lax.all_to_all(squares, both, 0, 0, tiled=True)  12.6 us
    all_to_all x1, starting transfers between devices, to_chips(): lax.all_to_all(x.reshape(-1, ROWS, pw), ('ex', 'basis'), 0, 0, tiled=True)  11.5 us
    pallas_call x1, Pallas kernels, turned(): pl.pallas_call(turn_kernel, grid=(local,), in_specs=[pl.BlockSpec((1, wid...  8.4 us
    pallas_call x1, Pallas kernels, rotated_grads(): pl.pallas_call(rot_grad_kernel, grid_spec=pltpu.PrefetchScalarGridSpec(nu...  6.05 us
    pallas_call x1, Pallas kernels, ex_gradients(): pl.pallas_call(second_kernel, in_specs=in_vmem(len(act) + 4), out_specs=i...  5.69 us
    all_to_all x1, starting transfers between devices, per_device(): lax.all_to_all(jnp.broadcast_to(lam, parts.shape), both, 0, 0, tiled=True)  4.51 us
  transfers between devices with their start and end apart: 5, of which 4 were waited for; matrix products, arithmetic and copies ran while one was open for 1% of the time, Pallas kernels for 14%

profile of v2, /device:TPU:1, one launch (start us, length us, event | category | flops | bytes accessed | tf_op | source)
XLA Modules:
  0.0 114.5 jit_solution(6398201049076331427)
XLA Ops:
  0.0 3.1 %shard_map.64 = (bf16[2,64,24,128]{3,2,1,0:T(8,128)(2,1)}, s32[1]{0:T(128)}) custom-call(s32[4]{0:T(128)} %owners_ref.3, bf16[4,60,24,128]{3,2,1,0:T(8,128)(2,1)} %bitcast.14), custom_call_target="tpu_custom_call" | custom-call | tf_op jit(solution)/shard_map/pallas_call | solution.py:48
  3.2 11.5 %all-to-all-start.1 = ((bf16[128,24,128]{2,1,0:T(8,128)(2,1)}), bf16[128,24,128]{2,1,0:T(8,128)(2,1)S(1)}, u32[]{:S(2)}, u32[]{:S(2)}) async-start(bf16[128,24,128]{2,1,0:T(8,128)(2,1)} %bitcast.17), calls=%async_computation.1 | async-start | bytes 1572864 | tf_op jit(solution)/shard_map/all_to_all | solution.py:301
  15.3 0.0 copy-start.6
  15.3 0.0 copy-start.8
  15.3 8.4 %shard_map.65 = (bf16[256,2880]{1,0:T(8,128)(2,1)}, bf16[256,2880]{1,0:T(8,128)(2,1)}, bf16[256,2880]{1,0:T(8,128)(2,1)}, bf16[256,2880]{1,0:T(8,128)(2,1)}, bf1...) custom-call(bf16[2,2880,768]{2,1,0:T(8,128)(2,1)} %bitcast.12), custom_call_target="tpu_custom_call" | custom-call | bytes 17694720 | tf_op jit(solution)/shard_map/pallas_call | solution.py:154
  23.7 0.0 copy-done.6
  23.7 0.0 copy-done.8
  23.7 0.0 copy-start.10
  23.7 6.1 %shard_map.66.refs_3_.refs_6_ = bf16[2,256,768]{2,1,0:T(8,128)(2,1)S(1)} custom-call(s32[2]{0:T(128)S(1)} %copy-done.8, bf16[2880,256]{1,0:T(8,128)(2,1)S(1)} %copy-done.6, bf16[2,2880,768]{2,1,0:T(8,128)(2,1)} %bitcast.13), custom_call_target="tpu_custom_call" | custom-call | flops 2264924160 | bytes 8847360 | tf_op jit(solution)/shard_map/pallas_call | solution.py:120
  29.8 0.9 all-to-all-done.1
  30.7 0.0 copy-done.9
  30.7 0.0 copy-done.10
  30.7 0.0 copy-start.2
  30.7 0.8 shard_map.67
  31.5 0.0 copy-start
  31.6 33.3 %all_to_all.24.refs_4_.refs_7_ = bf16[64,2,48,128]{3,2,1,0:T(8,128)(2,1)S(1)} all-to-all(bf16[64,2,48,128]{3,2,1,0:T(8,128)(2,1)S(1)} %shard_map.67), channel_id=1, replica_groups=mesh['basis'=64,'ex'=2] {'basis'}, dimensions={0} | all-to-all | bytes 3145728 | tf_op jit(solution)/shard_map/all_to_all | solution.py:317
  64.9 1.8 %collective-permute-start = (bf16[64,2,48,128]{3,2,1,0:T(8,128)(2,1)S(1)}, bf16[64,2,48,128]{3,2,1,0:T(8,128)(2,1)S(1)}, u32[]{:S(2)}, u32[]{:S(2)}) collective-permute-start(bf16[64,2,48,128]{3,2,1,0:T(8,128)(2,1)S(1)} %all_to_all.24.refs_4_.refs_7_), channel_id=1, source_target_pairs={{0,1},{1,0},{2,3},{3,2},{4,5},{5,4},{6,7},{7,6},{8,9},{9,8},{10,11... | collective-permute-start | bytes 4718600 | tf_op jit(solution)/shard_map/ppermute | solution.py:320
  66.7 0.0 copy-done
  66.7 1.7 %shard_map.68.refs_9_ = f32[256,256]{1,0:T(8,128)S(1)} custom-call(bf16[256,2880]{1,0:T(8,128)(2,1)S(1)} %copy-done, bf16[256,2880]{1,0:T(8,128)(2,1)S(1)} %copy-done.1, bf16[256,2880]{1,0:T(8,128)(2,1)S(1)} %copy-done.2, bf16[2,256,768]{2,1,0:T(8,128)(2,1)S(1)} %shard_map.66.refs_3_.refs_6_, bf16[64,2,48,128]{3,2,1,0:T(8,128)(2,1)S(1)} %all_to_all.24.refs_4_.refs_7_), custom_call_target="tpu_custom_call" | custom-call | flops 1132462080 | bytes 4423680 | tf_op jit(solution)/shard_map/pallas_call | solution.py:222
  68.4 1.3 %collective-permute-done.refs_8_ = bf16[64,2,48,128]{3,2,1,0:T(8,128)(2,1)S(1)} collective-permute-done((bf16[64,2,48,128]{3,2,1,0:T(8,128)(2,1)S(1)}, bf16[64,2,48,128]{3,2,1,0:T(8,128)(2,1)S(1)}, u32[]{:S(2)}, u32[]{:S(2)}) %collective-permute-start) | collective-permute-done | bytes 1572896 | tf_op jit(solution)/shard_map/ppermute | solution.py:320
  69.8 0.0 copy-done.3
  69.8 0.0 copy-done.5
  69.8 5.7 %shard_map.69 = (f32[2,2,128,256]{3,2,1,0:T(8,128)}, f32[2,2,128,256]{3,2,1,0:T(8,128)}, f32[128,8,128]{2,1,0:T(8,128)}) custom-call(bf16[256,2880]{1,0:T(8,128)(2,1)S(1)} %copy-done, bf16[256,2880]{1,0:T(8,128)(2,1)S(1)} %copy-done.1, bf16[256,2880]{1,0:T(8,128)(2,1)S(1)} %copy-done.2, bf16[256,2880]{1,0:T(8,128)(2,1)S(1)} %copy-done.3, ...), custom_call_target="tpu_custom_call" | custom-call | flops 3397386240 | bytes 13271040 | tf_op jit(solution)/shard_map/pallas_call | solution.py:231
  75.5 4.3 %all-to-all-start.3 = ((f32[128,8,128]{2,1,0:T(8,128)}), f32[128,8,128]{2,1,0:T(8,128)S(1)}, u32[]{:S(2)}, u32[]{:S(2)}) async-start(f32[128,8,128]{2,1,0:T(8,128)} %get-tuple-element.51), calls=%async_computation.3 | async-start | bytes 1048576 | tf_op jit(solution)/shard_map/all_to_all | solution.py:324
  79.7 1.1 %collective-permute-start.1 = (f32[2,2,128,256]{3,2,1,0:T(8,128)}, f32[2,2,128,256]{3,2,1,0:T(8,128)S(1)}, u32[]{:S(2)}, u32[]{:S(2)}) collective-permute-start(f32[2,2,128,256]{3,2,1,0:T(8,128)} %get-tuple-element.53), channel_id=1, source_target_pairs={{0,1},{1,0},{2,3},{3,2},{4,5},{5,4},{6,7},{7,6},{8,9},{9,8},{10,11... | collective-permute-start | bytes 1572872 | tf_op jit(solution)/shard_map/ppermute | solution.py:322
  80.9 12.6 %all-to-all-done.3 = f32[128,8,128]{2,1,0:T(8,128)S(1)} async-done(((f32[128,8,128]{2,1,0:T(8,128)}), f32[128,8,128]{2,1,0:T(8,128)S(1)}, u32[]{:S(2)}, u32[]{:S(2)}) %all-to-all-start.3) | async-done | bytes 524320 | tf_op jit(solution)/shard_map/all_to_all | solution.py:324
  93.4 0.1 reduce_sum.9
  93.6 0.8 broadcast_in_dim.2
  94.4 4.5 %all-to-all-start.4 = ((f32[128,8,128]{2,1,0:T(8,128)}), f32[128,8,128]{2,1,0:T(8,128)S(1)}, u32[]{:S(2)}, u32[]{:S(2)}) async-start(f32[128,8,128]{2,1,0:T(8,128)} %broadcast_in_dim.2), calls=%async_computation.4 | async-start | bytes 1048576 | tf_op jit(solution)/shard_map/all_to_all | solution.py:326
  98.9 0.0 collective-permute-done.1.got_ref
  98.9 13.7 %all-to-all-done.4.lam_ref = f32[128,8,128]{2,1,0:T(8,128)S(1)} async-done(((f32[128,8,128]{2,1,0:T(8,128)}), f32[128,8,128]{2,1,0:T(8,128)S(1)}, u32[]{:S(2)}, u32[]{:S(2)}) %all-to-all-start.4) | async-done | bytes 524320 | tf_op jit(solution)/shard_map/all_to_all | solution.py:326
  112.7 1.9 %shard_map.70 = f32[4,128,512]{2,1,0:T(8,128)} custom-call(f32[128,8,128]{2,1,0:T(8,128)S(1)} %all-to-all-done.4.lam_ref, f32[2,2,128,256]{3,2,1,0:T(8,128)S(1)} %copy-done.7, f32[2,2,128,256]{3,2,1,0:T(8,128)S(1)} %collective-permute-done.1.got_ref), custom_call_target="tpu_custom_call" | custom-call | tf_op jit(solution)/shard_map/pallas_call | solution.py:280
  (13 shorter events, 0.0 us)
Async XLA Ops:
  3.2 27.5 %all-to-all-start.1 = ((bf16[128,24,128]{2,1,0:T(8,128)(2,1)}), bf16[128,24,128]{2,1,0:T(8,128)(2,1)S(1)}, u32[]{:S(2)}, u32[]{:S(2)}) async-start(bf16[128,24,128]{2,1,0:T(8,128)(2,1)} %bitcast.17), calls=%async_computation.1 | async-start | bytes 1572864 | tf_op jit(solution)/shard_map/all_to_all | solution.py:301
  15.3 8.4 %copy-start.6 = (bf16[2880,256]{1,0:T(8,128)(2,1)S(1)}, bf16[2880,256]{1,0:T(8,128)(2,1)}, u32[]{:S(2)}) copy-start(bf16[2880,256]{1,0:T(8,128)(2,1)} %basis_ref.1) | copy-start | bytes 4423684
  15.3 8.4 %copy-start.8 = (s32[2]{0:T(128)S(1)}, s32[2]{0:T(128)}, u32[]{:S(2)}) copy-start(s32[2]{0:T(128)} %count_ref.1) | copy-start | bytes 28
  23.7 7.0 %copy-start.9 = (bf16[1,4,1440,128]{3,2,1,0:T(8,128)(2,1)S(1)}, bf16[1,4,1440,128]{3,2,1,0:T(8,128)(2,1)}, u32[]{:S(2)}) copy-start(bf16[1,4,1440,128]{3,2,1,0:T(8,128)(2,1)} %param.11) | copy-start | bytes 4423684
  23.7 7.0 %copy-start.10 = (s32[4]{0:T(128)S(1)}, s32[4]{0:T(128)}, u32[]{:S(2)}) copy-start(s32[4]{0:T(128)} %owners_ref.3) | copy-start | bytes 52
  30.7 36.0 %copy-start.2 = (bf16[256,2880]{1,0:T(8,128)(2,1)S(1)}, bf16[256,2880]{1,0:T(8,128)(2,1)}, u32[]{:S(2)}) copy-start(bf16[256,2880]{1,0:T(8,128)(2,1)} %get-tuple-element.43.refs_2_) | copy-start | bytes 4423684
  31.5 35.2 %copy-start = (bf16[256,2880]{1,0:T(8,128)(2,1)S(1)}, bf16[256,2880]{1,0:T(8,128)(2,1)}, u32[]{:S(2)}) copy-start(bf16[256,2880]{1,0:T(8,128)(2,1)} %get-tuple-element.41.refs_0_) | copy-start | bytes 4423684
  31.5 35.2 %copy-start.1 = (bf16[256,2880]{1,0:T(8,128)(2,1)S(1)}, bf16[256,2880]{1,0:T(8,128)(2,1)}, u32[]{:S(2)}) copy-start(bf16[256,2880]{1,0:T(8,128)(2,1)} %get-tuple-element.42.refs_1_) | copy-start | bytes 4423684
  64.9 4.9 %copy-start.3 = (bf16[256,2880]{1,0:T(8,128)(2,1)S(1)}, bf16[256,2880]{1,0:T(8,128)(2,1)}, u32[]{:S(2)}) copy-start(bf16[256,2880]{1,0:T(8,128)(2,1)} %get-tuple-element.44.refs_3_) | copy-start | bytes 4423684
  64.9 4.9 %copy-start.4 = (bf16[256,2880]{1,0:T(8,128)(2,1)S(1)}, bf16[256,2880]{1,0:T(8,128)(2,1)}, u32[]{:S(2)}) copy-start(bf16[256,2880]{1,0:T(8,128)(2,1)} %get-tuple-element.45.refs_4_) | copy-start | bytes 4423684
  64.9 4.9 %copy-start.5 = (bf16[256,2880]{1,0:T(8,128)(2,1)S(1)}, bf16[256,2880]{1,0:T(8,128)(2,1)}, u32[]{:S(2)}) copy-start(bf16[256,2880]{1,0:T(8,128)(2,1)} %get-tuple-element.46.refs_5_) | copy-start | bytes 4423684
  64.9 4.9 %collective-permute-start = (bf16[64,2,48,128]{3,2,1,0:T(8,128)(2,1)S(1)}, bf16[64,2,48,128]{3,2,1,0:T(8,128)(2,1)S(1)}, u32[]{:S(2)}, u32[]{:S(2)}) collective-permute-start(bf16[64,2,48,128]{3,2,1,0:T(8,128)(2,1)S(1)} %all_to_all.24.refs_4_.refs_7_), channel_id=1, source_target_pairs={{0,1},{1,0},{2,3},{3,2},{4,5},{5,4},{6,7},{7,6},{8,9},{9,8},{10,11... | collective-permute-start | bytes 4718600 | tf_op jit(solution)/shard_map/ppermute | solution.py:320
  75.5 37.2 %copy-start.7 = (f32[2,2,128,256]{3,2,1,0:T(8,128)S(1)}, f32[2,2,128,256]{3,2,1,0:T(8,128)}, u32[]{:S(2)}) copy-start(f32[2,2,128,256]{3,2,1,0:T(8,128)} %get-tuple-element.52.keep_ref) | copy-start | bytes 1572868
  75.5 18.0 %all-to-all-start.3 = ((f32[128,8,128]{2,1,0:T(8,128)}), f32[128,8,128]{2,1,0:T(8,128)S(1)}, u32[]{:S(2)}, u32[]{:S(2)}) async-start(f32[128,8,128]{2,1,0:T(8,128)} %get-tuple-element.51), calls=%async_computation.3 | async-start | bytes 1048576 | tf_op jit(solution)/shard_map/all_to_all | solution.py:324
  79.7 19.2 %collective-permute-start.1 = (f32[2,2,128,256]{3,2,1,0:T(8,128)}, f32[2,2,128,256]{3,2,1,0:T(8,128)S(1)}, u32[]{:S(2)}, u32[]{:S(2)}) collective-permute-start(f32[2,2,128,256]{3,2,1,0:T(8,128)} %get-tuple-element.53), channel_id=1, source_target_pairs={{0,1},{1,0},{2,3},{3,2},{4,5},{5,4},{6,7},{7,6},{8,9},{9,8},{10,11... | collective-permute-start | bytes 1572872 | tf_op jit(solution)/shard_map/ppermute | solution.py:322
  94.4 18.2 %all-to-all-start.4 = ((f32[128,8,128]{2,1,0:T(8,128)}), f32[128,8,128]{2,1,0:T(8,128)S(1)}, u32[]{:S(2)}, u32[]{:S(2)}) async-start(f32[128,8,128]{2,1,0:T(8,128)} %broadcast_in_dim.2), calls=%async_computation.4 | async-start | bytes 1048576 | tf_op jit(solution)/shard_map/all_to_all | solution.py:326

commit v3 on v2

--- a/solution.py
+++ b/solution.py
@@ -18,7 +18,7 @@
     return [pl.BlockSpec(memory_space=pltpu.VMEM)] * n
 
 
-def lay_kernel(cuts, owners_ref, x_ref, o_ref, shared_ref, held, sems):
+def lay_kernel(cuts, owners_ref, x_ref, o_ref, held, sems):
     pairs, blocks = held.shape[:2]
     step = blocks // cuts
     me = lax.axis_index("basis")
@@ -33,8 +33,6 @@
             gives.append(pltpu.make_async_copy(held.at[p, at], o_ref.at[p, at], sems.at[1, k]))
     for c in takes:
         c.start()
-    shared = [jnp.where(owners_ref[2 * p] == owners_ref[2 * p + 1], 1, 0) for p in range(pairs)]
-    shared_ref[0] = sum(shared)
     for c, d in zip(takes, gives):
         c.wait()
         d.start()
@@ -48,11 +46,8 @@
     return pl.pallas_call(
         functools.partial(lay_kernel, cuts),
         in_specs=[pl.BlockSpec(memory_space=pltpu.SMEM), pl.BlockSpec(memory_space=pl.ANY)],
-        out_specs=[pl.BlockSpec(memory_space=pl.ANY), pl.BlockSpec(memory_space=pltpu.SMEM)],
-        out_shape=[
-            pltpu.HBM((pairs, n_basis, rows, width), slots.dtype),
-            jax.ShapeDtypeStruct((1,), jnp.int32),
-        ],
+        out_specs=pl.BlockSpec(memory_space=pl.ANY),
+        out_shape=pltpu.HBM((pairs, n_basis, rows, width), slots.dtype),
         scratch_shapes=[
             pltpu.VMEM((pairs, blocks, rows, width), slots.dtype),
             pltpu.SemaphoreType.DMA((2, pairs * cuts)),
@@ -137,61 +132,77 @@
     )(token_count, grad_basis, x)
 
 
-def turn_kernel(x_ref, *o_refs):
-    parts = x_ref.shape[2] // TT
-    for i, o_ref in enumerate(o_refs):
-
-        @pl.when(pl.program_id(0) == i // parts)
-        def _():
-            x = x_ref[0, :, pl.ds(i % parts * TT, TT)].reshape(2, -1, ROWS, TT)
-            o_ref[...] = jnp.swapaxes(x, 0, 1).reshape(-1, TT).T
-
-
-def turned(activations):
-    local, tok, width = activations.shape
+def take_kernel(owners_ref, x_ref, o_ref, shared_ref, held, sems):
+    cuts = sems.shape[1]
+    step = o_ref.shape[0] // cuts
+    takes, gives = [], []
+    for i in range(cuts):
+        at = pl.ds(i * step, step)
+        takes.append(pltpu.make_async_copy(x_ref.at[0, at], held.at[at], sems.at[0, i]))
+        gives.append(pltpu.make_async_copy(held.at[at], o_ref.at[at], sems.at[1, i]))
+    for c in takes:
+        c.start()
+    shared = [owners_ref[p] == owners_ref[p + 1] for p in range(0, owners_ref.shape[0], 2)]
+    shared_ref[0] = sum(jnp.where(same, 1, 0) for same in shared)
+    for c, d in zip(takes, gives):
+        c.wait()
+        d.start()
+    for d in gives:
+        d.wait()
+
+
+def first_example(owners, activations):
+    _, tok, width = activations.shape
     x = pltpu.with_memory_space_constraint(jnp.swapaxes(activations, 1, 2), pltpu.HBM)
-    count = local * tok // TT
-    return pl.pallas_call(
-        turn_kernel,
-        grid=(local,),
-        in_specs=[pl.BlockSpec((1, width, tok), lambda n: (n, 0, 0))],
-        out_specs=[pl.BlockSpec((TT, width), lambda n: (0, 0))] * count,
-        out_shape=[pltpu.HBM((TT, width), BF16)] * count,
-        compiler_params=pltpu.CompilerParams(vmem_limit_bytes=40 << 20),
-        cost_estimate=pl.CostEstimate(flops=0, transcendentals=0, bytes_accessed=4 * local * tok * width),
-    )(x)
+    return pl.pallas_call(
+        take_kernel,
+        in_specs=[pl.BlockSpec(memory_space=pltpu.SMEM), pl.BlockSpec(memory_space=pl.ANY)],
+        out_specs=[pl.BlockSpec(memory_space=pl.ANY), pl.BlockSpec(memory_space=pltpu.SMEM)],
+        out_shape=[pltpu.HBM((width, tok), BF16), jax.ShapeDtypeStruct((1,), jnp.int32)],
+        scratch_shapes=[pltpu.VMEM((width, tok), BF16), pltpu.SemaphoreType.DMA((2, 6))],
+        compiler_params=pltpu.CompilerParams(vmem_limit_bytes=12 << 20),
+        cost_estimate=pl.CostEstimate(flops=0, transcendentals=0, bytes_accessed=4 * tok * width),
+    )(owners, x)
 
 
 def pair_of_panels(ref, width):
     senders = width // ref.shape[2]
-    return jnp.concatenate([ref[pl.ds(0, senders), k].reshape(width, 128) for k in range(2)], axis=1)
-
-
-def rotate(act_refs, pair, rot, slot):
-    for t, act_ref in enumerate(act_refs):
-        rot[slot, pl.ds(t * TT, TT)] = jnp.dot(act_ref[...], pair, preferred_element_type=F32).astype(BF16)
-
-
-def first_kernel(*refs):
-    *act_refs, rg_ref, basis_ref, ex_ref, rot = refs
-    rotate(act_refs, pair_of_panels(basis_ref, act_refs[0].shape[1]), rot, 0)
-    ex_ref[...] = jnp.dot(rg_ref[0], rot[0], preferred_element_type=F32)
+    panels = []
+    for k in range(2):
+        x = ref[pl.ds(0, senders), k].reshape(senders, 2, ROWS, 128)
+        panels.append(jnp.swapaxes(x, 0, 1).reshape(width, 128))
+    return jnp.concatenate(panels, axis=1).T
+
+
+def rotate(act_ref, pair_ref, rot, slot):
+    for t in range(0, act_ref.shape[1], TT):
+        at = pl.ds(t, TT)
+        rot[slot, :, at] = jnp.dot(pair_ref[...], act_ref[:, at], preferred_element_type=F32).astype(BF16)
+
+
+def gradients(rg, rot):
+    return lax.dot_general(rg, rot, (((1,), (1,)), ((), ())), preferred_element_type=F32)
+
+
+def first_kernel(act_ref, rg_ref, basis_ref, ex_ref, pair_ref, rot):
+    pair_ref[...] = pair_of_panels(basis_ref, act_ref.shape[0])
+    rotate(act_ref, pair_ref, rot, 0)
+    ex_ref[...] = gradients(rg_ref[0], rot[0])
 
 
 def second_kernel(*refs):
-    *act_refs, rg_ref, mine_ref, other_ref, own0_ref, keep_ref, send_ref, sq_ref, rot, own_ref, ex_ref = refs
+    act0_ref, act1_ref, rg_ref, mine_ref, other_ref, own0_ref, keep_ref, send_ref, sq_ref, rot, own_ref, ex_ref, pair_ref = refs
     e = lax.axis_index("ex")
     local, dirs, cols = own_ref.shape
     mid = dirs // 2
-    parts, width = len(act_refs) // local, act_refs[0].shape[1]
-    rotate(act_refs[parts:], pair_of_panels(mine_ref, width), rot, 0)
-    pair = pair_of_panels(other_ref, width)
-    rotate(act_refs[:parts], pair, rot, 1)
-    rotate(act_refs[parts:], pair, rot, 2)
+    rotate(act1_ref, mine_ref, rot, 0)
+    pair_ref[...] = pair_of_panels(other_ref, act0_ref.shape[0])
+    rotate(act0_ref, pair_ref, rot, 1)
+    rotate(act1_ref, pair_ref, rot, 2)
     own_ref[0] = own0_ref[...]
-    own_ref[1] = jnp.dot(rg_ref[1], rot[0], preferred_element_type=F32)
+    own_ref[1] = gradients(rg_ref[1], rot[0])
     for n in range(local):
-        ex_ref[n] = jnp.dot(rg_ref[n], rot[1 + n], preferred_element_type=F32)
+        ex_ref[n] = gradients(rg_ref[n], rot[1 + n])
     here, there = (pl.ds(pl.multiple_of(x * mid, 8), mid) for x in (e, 1 - e))
     for n in range(local):
         for side, src in enumerate((own_ref, ex_ref)):
@@ -211,26 +222,25 @@
 
 def ex_gradients(act, rg, mine, other):
     local, dirs, tok = rg.shape
-    width = act[0].shape[1]
-    parts = len(act) // local
+    width = act[0].shape[0]
 
     def cost(count):
         return pl.CostEstimate(
             flops=2 * count * tok * width * 256, transcendentals=0, bytes_accessed=2 * count * tok * width
         )
 
-    own = pl.pallas_call(
+    own, pair = pl.pallas_call(
         first_kernel,
-        in_specs=in_vmem(parts + 2),
-        out_specs=pl.BlockSpec(memory_space=pltpu.VMEM),
-        out_shape=pltpu.VMEM((dirs, 256), F32),
-        scratch_shapes=[pltpu.VMEM((1, tok, 256), BF16)],
+        in_specs=in_vmem(3),
+        out_specs=in_vmem(2),
+        out_shape=[pltpu.VMEM((dirs, 256), F32), pltpu.VMEM((256, width), BF16)],
+        scratch_shapes=[pltpu.VMEM((1, 256, tok), BF16)],
         compiler_params=pltpu.CompilerParams(vmem_limit_bytes=16 << 20),
         cost_estimate=cost(1),
-    )(*act[:parts], rg, mine)
+    )(act[0], rg, mine)
     return pl.pallas_call(
         second_kernel,
-        in_specs=in_vmem(len(act) + 4),
+        in_specs=in_vmem(6),
         out_specs=in_vmem(3),
         out_shape=[
             pltpu.HBM((local, 2, dirs // 2, 256), F32),
@@ -238,26 +248,30 @@
             pltpu.HBM((dirs * 512 // 1024, 8, 128), F32),
         ],
         scratch_shapes=[
-            pltpu.VMEM((3, tok, 256), BF16),
+            pltpu.VMEM((3, 256, tok), BF16),
             pltpu.VMEM((local, dirs, 256), F32),
             pltpu.VMEM((local, dirs, 256), F32),
+            pltpu.VMEM((256, width), BF16),
         ],
         compiler_params=pltpu.CompilerParams(vmem_limit_bytes=16 << 20),
         cost_estimate=cost(3),
-    )(*act, rg, mine, other, own)
-
-
-def scale_kernel(lam_ref, keep_ref, got_ref, o_ref, inv):
+    )(*act, rg, pair, other, own)
+
+
+def scale_kernel(lam_ref, keep_ref, got_ref, o_ref, inv, held, sem):
     e, i = lax.axis_index("ex"), pl.program_id(0)
     local = keep_ref.shape[0]
     tiles, across = lam_ref.shape[0] // 2, 4
 
     @pl.when(i == 0)
     def _():
+        fetch = pltpu.make_async_copy(keep_ref, held, sem)
+        fetch.start()
         damp = jnp.sum(jnp.sum(lam_ref[...], axis=0), keepdims=True) * (0.1 / lam_ref.size)
         for j in range(tiles):
             r, c = j // across, j % across
             inv[pl.ds(8 * r, 8), pl.ds(128 * c, 128)] = 1.0 / (lam_ref[2 * j + e] + damp)
+        fetch.wait()
 
     for core in range(2):
         for j in range(local):
@@ -265,7 +279,7 @@
 
                 @pl.when((i == core * local + j) & (own == (e == core)))
                 def _():
-                    src = keep_ref if own else got_ref
+                    src = held if own else got_ref
                     for side in range(2):
                         at = pl.ds(256 * (core if side == 0 else 1 - core), 256)
                         o_ref[0, :, at] = src[j, side] * inv[:, at]
@@ -280,12 +294,12 @@
     return pl.pallas_call(
         scale_kernel,
         grid=(2 * local,),
-        in_specs=[whole(lam), whole(keep), whole(got)],
+        in_specs=[whole(lam), pl.BlockSpec(memory_space=pl.ANY), whole(got)],
         out_specs=pl.BlockSpec((1, dirs, 512), lambda i: (i, 0, 0)),
-        scratch_shapes=[pltpu.VMEM((dirs, 512), F32)],
+        scratch_shapes=[pltpu.VMEM((dirs, 512), F32), pltpu.VMEM(keep.shape, F32), pltpu.SemaphoreType.DMA],
         out_shape=jax.ShapeDtypeStruct((2 * local, dirs, 512), F32),
         compiler_params=pltpu.CompilerParams(vmem_limit_bytes=8 << 20),
-    )(lam, keep, got)
+    )(lam, pltpu.with_memory_space_constraint(keep, pltpu.HBM), got)
 
 
 def per_device(activations, out_grads, grad_basis, panel_store, owners, token_count):
@@ -295,16 +309,17 @@
     blocks = half // ROWS
 
     slots = panel_store.reshape(panels, blocks, ROWS, pw)
-    sent, shared = laid(owners, slots, n_basis)
+    sent = laid(owners, slots, n_basis)
 
     def to_chips(x):
         got = lax.all_to_all(x.reshape(-1, ROWS, pw), ("ex", "basis"), 0, 0, tiled=True)
         return got.reshape(2, n_basis, ROWS, pw)
 
     arrived = to_chips(sent)
-    act = turned(activations)
+    act0, shared = first_example(owners, activations)
     rg = rotated_grads(token_count, grad_basis, out_grads)
-    arrived, slots, act, rg = lax.optimization_barrier((arrived, slots, act, rg))
+    arrived, slots, act0, rg = lax.optimization_barrier((arrived, slots, act0, rg))
+    act = [act0, activations[1].T]
 
     def second_panels(slots):
         second = to_chips(jnp.pad(slots[1::2], ((0, 0), (0, n_basis - blocks), (0, 0), (0, 0))))

time: 115 us -> 113 us (0.983)
  blocking collectives: 33.3 us -> 29.9 us
  Pallas kernels: 27.7 us -> 24.7 us
  local copies, waits for them, and re-layouts: 0.88 us -> 3.41 us
  waiting for transfers between devices: 28.5 us -> 30.6 us
    all_to_all x1, waiting for transfers between devices: 0.87 us -> 4.29 us  [to_chips(): lax.all_to_all(x.reshape(-1, ROWS, pw), ('ex', 'basis'), 0, 0, tiled=True)]
    all_to_all x1, blocking collectives: 33.3 us -> 29.9 us  [per_device(): lax.all_to_all(picked(owners, arrived, second), 'basis', 0, 0, tiled=True)]
    transpose x0 -> x1, local copies, waits for them, and re-layouts: none -> 2.54 us  [per_device(): act = [act0, activations[1].T]]
    pallas_call x4, Pallas kernels: 17.7 us -> 15.2 us  [the longest x1 5.8 us: ex_gradients(): pl.pallas_call(second_kernel, in_specs=in_vmem(6), out_specs=in_vmem(3),...]
    ppermute x1, waiting for transfers between devices: 1.34 us -> 0.01 us  [per_device(): other = lax.ppermute(mine, 'ex', swap)]
  transfers between devices with their start and end apart: 5 -> 5, of which waited for: 4 -> 3; matrix products, arithmetic and copies ran while one was open for 1% -> 3% of each run, Pallas kernels for 14% -> 11%
where the time goes in v3:
time: 113 us; the launch traced here: 112 us
  waiting for transfers between devices  30.6 us (27%)
  blocking collectives  29.9 us (26%)
  Pallas kernels  24.7 us (22%)
  starting transfers between devices  23 us (20%)
  local copies, waits for them, and re-layouts  3.41 us (3%)
    all_to_all x1, blocking collectives, per_device(): lax.all_to_all(picked(owners, arrived, second), 'basis', 0, 0, tiled=True)  29.9 us
    all_to_all x1, waiting for transfers between devices, per_device(): lax.all_to_all(jnp.broadcast_to(lam, parts.shape), both, 0, 0, tiled=True)  13.7 us
    all_to_all x1, waiting for transfers between devices, per_device(): parts = lax.all_to_all(squares, both, 0, 0, tiled=True)  12.6 us
    all_to_all x1, starting transfers between devices, to_chips(): lax.all_to_all(x.reshape(-1, ROWS, pw), ('ex', 'basis'), 0, 0, tiled=True)  11.5 us
    pallas_call x1, Pallas kernels, rotated_grads(): pl.pallas_call(rot_grad_kernel, grid_spec=pltpu.PrefetchScalarGridSpec(nu...  6.05 us
    pallas_call x1, Pallas kernels, ex_gradients(): pl.pallas_call(second_kernel, in_specs=in_vmem(6), out_specs=in_vmem(3),...  5.8 us
    pallas_call x1, Pallas kernels, first_example(): pl.pallas_call(take_kernel, in_specs=[pl.BlockSpec(memory_space=pltpu.SME...  5.02 us
    all_to_all x1, starting transfers between devices, per_device(): lax.all_to_all(jnp.broadcast_to(lam, parts.shape), both, 0, 0, tiled=True)  4.51 us
  transfers between devices with their start and end apart: 5, of which 3 were waited for; matrix products, arithmetic and copies ran while one was open for 3% of the time, Pallas kernels for 11%

profile of v3, /device:TPU:1, one launch (start us, length us, event | category | flops | bytes accessed | tf_op | source)
XLA Modules:
  0.0 112.5 jit_solution(3355394235177351265)
XLA Ops:
  0.0 2.6 %shard_map.64 = bf16[2,64,24,128]{3,2,1,0:T(8,128)(2,1)} custom-call(s32[4]{0:T(128)} %owners_ref.5, bf16[4,60,24,128]{3,2,1,0:T(8,128)(2,1)} %bitcast.20), custom_call_target="tpu_custom_call" | custom-call | tf_op jit(solution)/shard_map/pallas_call | solution.py:46
  2.6 11.5 %all-to-all-start.1 = ((bf16[128,24,128]{2,1,0:T(8,128)(2,1)}), bf16[128,24,128]{2,1,0:T(8,128)(2,1)S(1)}, u32[]{:S(2)}, u32[]{:S(2)}) async-start(bf16[128,24,128]{2,1,0:T(8,128)(2,1)} %bitcast.22), calls=%async_computation.1 | async-start | bytes 1572864 | tf_op jit(solution)/shard_map/all_to_all | solution.py:315
  14.1 0.0 copy-start
  14.2 0.0 copy-start.1
  14.2 5.0 %shard_map.65 = (bf16[2880,768]{1,0:T(8,128)(2,1)}, s32[1]{0:T(128)}) custom-call(s32[4]{0:T(128)} %owners_ref.5, bf16[2,2880,768]{2,1,0:T(8,128)(2,1)} %bitcast.18), custom_call_target="tpu_custom_call" | custom-call | bytes 8847360 | tf_op jit(solution)/shard_map/pallas_call | solution.py:157
  19.8 0.0 copy-done
  19.8 0.0 copy-done.1
  19.8 0.0 copy-start.2
  19.8 0.0 copy-start.3
  19.8 6.1 %shard_map.66.rg_ref.refs_2_ = bf16[2,256,768]{2,1,0:T(8,128)(2,1)S(1)} custom-call(s32[2]{0:T(128)S(1)} %copy-done.1, bf16[2880,256]{1,0:T(8,128)(2,1)S(1)} %copy-done, bf16[2,2880,768]{2,1,0:T(8,128)(2,1)} %bitcast.19), custom_call_target="tpu_custom_call" | custom-call | flops 2264924160 | bytes 8847360 | tf_op jit(solution)/shard_map/pallas_call | solution.py:115
  25.9 4.3 %all-to-all-done.1 = bf16[128,24,128]{2,1,0:T(8,128)(2,1)S(1)} async-done(((bf16[128,24,128]{2,1,0:T(8,128)(2,1)}), bf16[128,24,128]{2,1,0:T(8,128)(2,1)S(1)}, u32[]{:S(2)}, u32[]{:S(2)}) %all-to-all-start.1) | async-done | bytes 786464 | tf_op jit(solution)/shard_map/all_to_all | solution.py:315
  30.2 0.0 copy-done.2
  30.2 0.0 copy-done.3
  30.2 0.8 shard_map.67
  31.0 0.0 slice-start
  31.0 29.9 %all_to_all.24.basis_ref = bf16[64,2,48,128]{3,2,1,0:T(8,128)(2,1)S(1)} all-to-all(bf16[64,2,48,128]{3,2,1,0:T(8,128)(2,1)S(1)} %shard_map.67), channel_id=1, replica_groups=mesh['basis'=64,'ex'=2] {'basis'}, dimensions={0} | all-to-all | bytes 3145728 | tf_op jit(solution)/shard_map/all_to_all | solution.py:332
  60.9 1.8 %collective-permute-start = (bf16[64,2,48,128]{3,2,1,0:T(8,128)(2,1)S(1)}, bf16[64,2,48,128]{3,2,1,0:T(8,128)(2,1)S(1)}, u32[]{:S(2)}, u32[]{:S(2)}) collective-permute-start(bf16[64,2,48,128]{3,2,1,0:T(8,128)(2,1)S(1)} %all_to_all.24.basis_ref), channel_id=1, source_target_pairs={{0,1},{1,0},{2,3},{3,2},{4,5},{5,4},{6,7},{7,6},{8,9},{9,8},{10,11... | collective-permute-start | bytes 4718600 | tf_op jit(solution)/shard_map/ppermute | solution.py:335
  62.8 2.5 %slice_bitcast_fusion.refs_1_ = bf16[2880,768]{1,0:T(8,128)(2,1)S(1)} fusion(bf16[2,768,2880]{1,2,0:T(8,128)(2,1)} %param.8), kind=kLoop, calls=%fused_computation.1 | loop fusion | bytes 8847360 | tf_op jit(solution)/shard_map/transpose | solution.py:322
  65.3 0.0 slice-done
  65.3 0.0 slice-done.1
  65.3 1.7 %shard_map.68 = (f32[256,256]{1,0:T(8,128)S(1)}, bf16[256,2880]{1,0:T(8,128)(2,1)S(1)}) custom-call(bf16[2880,768]{1,0:T(8,128)(2,1)S(1)} %bitcast.16, bf16[2,256,768]{2,1,0:T(8,128)(2,1)S(1)} %shard_map.66.rg_ref.refs_2_, bf16[64,2,48,128]{3,2,1,0:T(8,128)(2,1)S(1)} %all_to_all.24.basis_ref), custom_call_target="tpu_custom_call" | custom-call | flops 1132462080 | bytes 4423680 | tf_op jit(solution)/shard_map/pallas_call | solution.py:232
  67.0 0.0 collective-permute-done.refs_4_
  67.1 5.8 %shard_map.69 = (f32[2,2,128,256]{3,2,1,0:T(8,128)}, f32[2,2,128,256]{3,2,1,0:T(8,128)}, f32[128,8,128]{2,1,0:T(8,128)}) custom-call(bf16[2880,768]{1,0:T(8,128)(2,1)S(1)} %bitcast.16, bf16[2880,768]{1,0:T(8,128)(2,1)S(1)} %slice_bitcast_fusion.refs_1_, bf16[2,256,768]{2,1,0:T(8,128)(2,1)S(1)} %shard_map.66.rg_ref.refs_2_, ...), custom_call_target="tpu_custom_call" | custom-call | flops 3397386240 | bytes 13271040 | tf_op jit(solution)/shard_map/pallas_call | solution.py:241
  72.9 4.0 %all-to-all-start.3 = ((f32[128,8,128]{2,1,0:T(8,128)}), f32[128,8,128]{2,1,0:T(8,128)S(1)}, u32[]{:S(2)}, u32[]{:S(2)}) async-start(f32[128,8,128]{2,1,0:T(8,128)} %get-tuple-element.33), calls=%async_computation.3 | async-start | bytes 1048576 | tf_op jit(solution)/shard_map/all_to_all | solution.py:339
  76.9 1.1 %collective-permute-start.1 = (f32[2,2,128,256]{3,2,1,0:T(8,128)}, f32[2,2,128,256]{3,2,1,0:T(8,128)S(1)}, u32[]{:S(2)}, u32[]{:S(2)}) collective-permute-start(f32[2,2,128,256]{3,2,1,0:T(8,128)} %get-tuple-element.35), channel_id=1, source_target_pairs={{0,1},{1,0},{2,3},{3,2},{4,5},{5,4},{6,7},{7,6},{8,9},{9,8},{10,11... | collective-permute-start | bytes 1572872 | tf_op jit(solution)/shard_map/ppermute | solution.py:337
  78.0 12.6 %all-to-all-done.3 = f32[128,8,128]{2,1,0:T(8,128)S(1)} async-done(((f32[128,8,128]{2,1,0:T(8,128)}), f32[128,8,128]{2,1,0:T(8,128)S(1)}, u32[]{:S(2)}, u32[]{:S(2)}) %all-to-all-start.3) | async-done | bytes 524320 | tf_op jit(solution)/shard_map/all_to_all | solution.py:339
  90.6 0.1 reduce_sum.9
  90.7 0.8 broadcast_in_dim.2
  91.6 4.5 %all-to-all-start.4 = ((f32[128,8,128]{2,1,0:T(8,128)}), f32[128,8,128]{2,1,0:T(8,128)S(1)}, u32[]{:S(2)}, u32[]{:S(2)}) async-start(f32[128,8,128]{2,1,0:T(8,128)} %broadcast_in_dim.2), calls=%async_computation.4 | async-start | bytes 1048576 | tf_op jit(solution)/shard_map/all_to_all | solution.py:341
  96.1 0.0 collective-permute-done.1.got_ref
  96.1 13.7 %all-to-all-done.4.lam_ref = f32[128,8,128]{2,1,0:T(8,128)S(1)} async-done(((f32[128,8,128]{2,1,0:T(8,128)}), f32[128,8,128]{2,1,0:T(8,128)S(1)}, u32[]{:S(2)}, u32[]{:S(2)}) %all-to-all-start.4) | async-done | bytes 524320 | tf_op jit(solution)/shard_map/all_to_all | solution.py:341
  109.8 2.6 %shard_map.70 = f32[4,128,512]{2,1,0:T(8,128)} custom-call(f32[128,8,128]{2,1,0:T(8,128)S(1)} %all-to-all-done.4.lam_ref, f32[2,2,128,256]{3,2,1,0:T(8,128)} %get-tuple-element.34.keep_ref, f32[2,2,128,256]{3,2,1,0:T(8,128)S(1)} %collective-permute-done.1.got_ref), custom_call_target="tpu_custom_call" | custom-call | tf_op jit(solution)/shard_map/pallas_call | solution.py:294
  (5 shorter events, 0.0 us)
Async XLA Ops:
  2.6 27.5 %all-to-all-start.1 = ((bf16[128,24,128]{2,1,0:T(8,128)(2,1)}), bf16[128,24,128]{2,1,0:T(8,128)(2,1)S(1)}, u32[]{:S(2)}, u32[]{:S(2)}) async-start(bf16[128,24,128]{2,1,0:T(8,128)(2,1)} %bitcast.22), calls=%async_computation.1 | async-start | bytes 1572864 | tf_op jit(solution)/shard_map/all_to_all | solution.py:315
  14.1 5.6 %copy-start = (bf16[2880,256]{1,0:T(8,128)(2,1)S(1)}, bf16[2880,256]{1,0:T(8,128)(2,1)}, u32[]{:S(2)}) copy-start(bf16[2880,256]{1,0:T(8,128)(2,1)} %basis_ref.1) | copy-start | bytes 4423684
  14.2 5.6 %copy-start.1 = (s32[2]{0:T(128)S(1)}, s32[2]{0:T(128)}, u32[]{:S(2)}) copy-start(s32[2]{0:T(128)} %count_ref.1) | copy-start | bytes 28
  19.8 10.4 %copy-start.2 = (bf16[1,4,1440,128]{3,2,1,0:T(8,128)(2,1)S(1)}, bf16[1,4,1440,128]{3,2,1,0:T(8,128)(2,1)}, u32[]{:S(2)}) copy-start(bf16[1,4,1440,128]{3,2,1,0:T(8,128)(2,1)} %param.11) | copy-start | bytes 4423684
  19.8 10.4 %copy-start.3 = (s32[4]{0:T(128)S(1)}, s32[4]{0:T(128)}, u32[]{:S(2)}) copy-start(s32[4]{0:T(128)} %owners_ref.5) | copy-start | bytes 52
  31.0 34.3 %slice-start = ((s8[4423680]{0:T(1024)(128)(4,1)}), s8[4194304]{0:T(1024)(128)(4,1)S(1)}, s32[]{:S(2)}) async-start(s8[4423680]{0:T(1024)(128)(4,1)} %bitcast.15), calls=%async_computation.5 | async-start | bytes 8388608
  60.9 4.4 %slice-start.1 = ((s8[4423680]{0:T(1024)(128)(4,1)}), s8[229376]{0:T(1024)(128)(4,1)S(1)}, s32[]{:S(2)}) async-start(s8[4423680]{0:T(1024)(128)(4,1)} %bitcast.15), calls=%async_computation.6 | async-start | bytes 458752
  60.9 6.1 %collective-permute-start = (bf16[64,2,48,128]{3,2,1,0:T(8,128)(2,1)S(1)}, bf16[64,2,48,128]{3,2,1,0:T(8,128)(2,1)S(1)}, u32[]{:S(2)}, u32[]{:S(2)}) collective-permute-start(bf16[64,2,48,128]{3,2,1,0:T(8,128)(2,1)S(1)} %all_to_all.24.basis_ref), channel_id=1, source_target_pairs={{0,1},{1,0},{2,3},{3,2},{4,5},{5,4},{6,7},{7,6},{8,9},{9,8},{10,11... | collective-permute-start | bytes 4718600 | tf_op jit(solution)/shard_map/ppermute | solution.py:335
  72.9 17.7 %all-to-all-start.3 = ((f32[128,8,128]{2,1,0:T(8,128)}), f32[128,8,128]{2,1,0:T(8,128)S(1)}, u32[]{:S(2)}, u32[]{:S(2)}) async-start(f32[128,8,128]{2,1,0:T(8,128)} %get-tuple-element.33), calls=%async_computation.3 | async-start | bytes 1048576 | tf_op jit(solution)/shard_map/all_to_all | solution.py:339
  76.9 19.2 %collective-permute-start.1 = (f32[2,2,128,256]{3,2,1,0:T(8,128)}, f32[2,2,128,256]{3,2,1,0:T(8,128)S(1)}, u32[]{:S(2)}, u32[]{:S(2)}) collective-permute-start(f32[2,2,128,256]{3,2,1,0:T(8,128)} %get-tuple-element.35), channel_id=1, source_target_pairs={{0,1},{1,0},{2,3},{3,2},{4,5},{5,4},{6,7},{7,6},{8,9},{9,8},{10,11... | collective-permute-start | bytes 1572872 | tf_op jit(solution)/shard_map/ppermute | solution.py:337
  91.6 18.2 %all-to-all-start.4 = ((f32[128,8,128]{2,1,0:T(8,128)}), f32[128,8,128]{2,1,0:T(8,128)S(1)}, u32[]{:S(2)}, u32[]{:S(2)}) async-start(f32[128,8,128]{2,1,0:T(8,128)} %broadcast_in_dim.2), calls=%async_computation.4 | async-start | bytes 1048576 | tf_op jit(solution)/shard_map/all_to_all | solution.py:341

commit v4 on v3

--- a/solution.py
+++ b/solution.py
@@ -9,7 +9,6 @@
 
 ROWS = 24
 TT = 256
-GT = 768
 F32 = jnp.float32
 BF16 = jnp.bfloat16
 
@@ -95,74 +94,53 @@
     )(owners, arrived, second)
 
 
-def rot_grad_kernel(count_ref, basis_ref, x_ref, o_ref, turned_basis):
-    n, t = pl.program_id(0), pl.program_id(1)
-    step = o_ref.shape[2]
-
-    @pl.when((n == 0) & (t == 0))
-    def _():
-        turned_basis[...] = basis_ref[...].T
-
-    rot = jnp.dot(turned_basis[...], x_ref[0], preferred_element_type=F32).astype(BF16)
-    live = t * step + lax.broadcasted_iota(jnp.int32, rot.shape, 1) < count_ref[n]
-    o_ref[0] = jnp.where(live, rot, jnp.zeros_like(rot))
-
-
-def rotated_grads(token_count, grad_basis, out_grads):
-    local, tok, width = out_grads.shape
-    dirs = grad_basis.shape[1]
-    x = pltpu.with_memory_space_constraint(jnp.swapaxes(out_grads, 1, 2), pltpu.HBM)
-    return pl.pallas_call(
-        rot_grad_kernel,
-        grid_spec=pltpu.PrefetchScalarGridSpec(
-            num_scalar_prefetch=1,
-            grid=(local, tok // GT),
-            in_specs=[
-                pl.BlockSpec((width, dirs), lambda n, t, count: (0, 0)),
-                pl.BlockSpec((1, width, GT), lambda n, t, count: (n, 0, t)),
-            ],
-            out_specs=pl.BlockSpec((1, dirs, GT), lambda n, t, count: (n, 0, t)),
-            scratch_shapes=[pltpu.VMEM((dirs, width), BF16)],
-        ),
-        out_shape=jax.ShapeDtypeStruct((local, dirs, tok), BF16),
-        compiler_params=pltpu.CompilerParams(vmem_limit_bytes=28 << 20),
-        cost_estimate=pl.CostEstimate(
-            flops=2 * local * tok * width * dirs, transcendentals=0, bytes_accessed=2 * local * tok * width
-        ),
-    )(token_count, grad_basis, x)
-
-
-def take_kernel(owners_ref, x_ref, o_ref, shared_ref, held, sems):
-    cuts = sems.shape[1]
-    step = o_ref.shape[0] // cuts
-    takes, gives = [], []
-    for i in range(cuts):
-        at = pl.ds(i * step, step)
-        takes.append(pltpu.make_async_copy(x_ref.at[0, at], held.at[at], sems.at[0, i]))
-        gives.append(pltpu.make_async_copy(held.at[at], o_ref.at[at], sems.at[1, i]))
-    for c in takes:
+def early_kernel(owners_ref, count_ref, basis_ref, grads_ref, act_ref, rg_ref, act0_ref, shared_ref, grads, held, sems):
+    local = grads.shape[0]
+    reads = [pltpu.make_async_copy(grads_ref.at[n], grads.at[n], sems.at[n]) for n in range(local)]
+    take = pltpu.make_async_copy(act_ref.at[0], held, sems.at[local])
+    give = pltpu.make_async_copy(held, act0_ref, sems.at[local + 1])
+    for c in (reads[0], take, *reads[1:]):
         c.start()
     shared = [owners_ref[p] == owners_ref[p + 1] for p in range(0, owners_ref.shape[0], 2)]
     shared_ref[0] = sum(jnp.where(same, 1, 0) for same in shared)
-    for c, d in zip(takes, gives):
-        c.wait()
-        d.start()
-    for d in gives:
-        d.wait()
-
-
-def first_example(owners, activations):
-    _, tok, width = activations.shape
-    x = pltpu.with_memory_space_constraint(jnp.swapaxes(activations, 1, 2), pltpu.HBM)
-    return pl.pallas_call(
-        take_kernel,
-        in_specs=[pl.BlockSpec(memory_space=pltpu.SMEM), pl.BlockSpec(memory_space=pl.ANY)],
-        out_specs=[pl.BlockSpec(memory_space=pl.ANY), pl.BlockSpec(memory_space=pltpu.SMEM)],
-        out_shape=[pltpu.HBM((width, tok), BF16), jax.ShapeDtypeStruct((1,), jnp.int32)],
-        scratch_shapes=[pltpu.VMEM((width, tok), BF16), pltpu.SemaphoreType.DMA((2, 6))],
-        compiler_params=pltpu.CompilerParams(vmem_limit_bytes=12 << 20),
-        cost_estimate=pl.CostEstimate(flops=0, transcendentals=0, bytes_accessed=4 * tok * width),
-    )(owners, x)
+    turned = basis_ref[...].T
+    for n in range(local):
+        reads[n].wait()
+        if n == 0:
+            take.wait()
+            give.start()
+        rot = jnp.dot(turned, grads[n], preferred_element_type=F32).astype(BF16)
+        live = lax.broadcasted_iota(jnp.int32, rot.shape, 1) < count_ref[n]
+        rg_ref[n] = jnp.where(live, rot, jnp.zeros_like(rot))
+    give.wait()
+
+
+def early(owners, token_count, grad_basis, out_grads, activations):
+    local, tok, width = out_grads.shape
+    dirs = grad_basis.shape[1]
+    grads, act = (
+        pltpu.with_memory_space_constraint(jnp.swapaxes(x, 1, 2), pltpu.HBM) for x in (out_grads, activations)
+    )
+    smem, hbm = pl.BlockSpec(memory_space=pltpu.SMEM), pl.BlockSpec(memory_space=pl.ANY)
+    return pl.pallas_call(
+        early_kernel,
+        in_specs=[smem, smem, *in_vmem(1), hbm, hbm],
+        out_specs=[*in_vmem(1), hbm, smem],
+        out_shape=[
+            jax.ShapeDtypeStruct((local, dirs, tok), BF16),
+            pltpu.HBM((width, tok), BF16),
+            jax.ShapeDtypeStruct((1,), jnp.int32),
+        ],
+        scratch_shapes=[
+            pltpu.VMEM((local, width, tok), BF16),
+            pltpu.VMEM((width, tok), BF16),
+            pltpu.SemaphoreType.DMA((local + 2,)),
+        ],
+        compiler_params=pltpu.CompilerParams(vmem_limit_bytes=28 << 20),
+        cost_estimate=pl.CostEstimate(
+            flops=2 * local * tok * width * dirs, transcendentals=0, bytes_accessed=4 * local * tok * width
+        ),
+    )(owners, token_count, grad_basis, grads, act)
 
 
 def pair_of_panels(ref, width):
@@ -316,8 +294,7 @@
         return got.reshape(2, n_basis, ROWS, pw)
 
     arrived = to_chips(sent)
-    act0, shared = first_example(owners, activations)
-    rg = rotated_grads(token_count, grad_basis, out_grads)
+    rg, act0, shared = early(owners, token_count, grad_basis, out_grads, activations)
     arrived, slots, act0, rg = lax.optimization_barrier((arrived, slots, act0, rg))
     act = [act0, activations[1].T]
 

time: 113 us -> 112 us (level)
  Pallas kernels: 24.7 us -> 22.3 us
  waiting for transfers between devices: 30.6 us -> 32.4 us
  blocking collectives: 29.9 us -> 28.4 us
    pallas_call x2 -> x1, Pallas kernels: 11.1 us -> 8.57 us  [early(): pl.pallas_call(early_kernel, in_specs=[smem, smem, *in_vmem(1), hbm, hbm]...]
    all_to_all x1, waiting for transfers between devices: 4.29 us -> 6.09 us  [to_chips(): lax.all_to_all(x.reshape(-1, ROWS, pw), ('ex', 'basis'), 0, 0, tiled=True)]
    all_to_all x1, blocking collectives: 29.9 us -> 28.4 us  [per_device(): lax.all_to_all(picked(owners, arrived, second), 'basis', 0, 0, tiled=True)]
  transfers between devices with their start and end apart: 5 -> 5, of which waited for: 3 -> 3; matrix products, arithmetic and copies ran while one was open for 3% -> 3% of each run, Pallas kernels for 11% -> 9%
where the time goes in v4:
time: 112 us; the launch traced here: 111 us
  waiting for transfers between devices  32.4 us (29%)
  blocking collectives  28.4 us (25%)
  starting transfers between devices  23.2 us (21%)
  Pallas kernels  22.3 us (20%)
  local copies, waits for them, and re-layouts  4.04 us (4%)
    all_to_all x1, blocking collectives, per_device(): lax.all_to_all(picked(owners, arrived, second), 'basis', 0, 0, tiled=True)  28.4 us
    all_to_all x1, waiting for transfers between devices, per_device(): lax.all_to_all(jnp.broadcast_to(lam, parts.shape), both, 0, 0, tiled=True)  13.7 us
    all_to_all x1, waiting for transfers between devices, per_device(): parts = lax.all_to_all(squares, both, 0, 0, tiled=True)  12.6 us
    all_to_all x1, starting transfers between devices, to_chips(): lax.all_to_all(x.reshape(-1, ROWS, pw), ('ex', 'basis'), 0, 0, tiled=True)  11.5 us
    pallas_call x1, Pallas kernels, early(): pl.pallas_call(early_kernel, in_specs=[smem, smem, *in_vmem(1), hbm, hbm]...  8.57 us
    all_to_all x1, waiting for transfers between devices, to_chips(): lax.all_to_all(x.reshape(-1, ROWS, pw), ('ex', 'basis'), 0, 0, tiled=True)  6.09 us
    pallas_call x1, Pallas kernels, ex_gradients(): pl.pallas_call(second_kernel, in_specs=in_vmem(6), out_specs=in_vmem(3),...  5.8 us
    all_to_all x1, starting transfers between devices, per_device(): lax.all_to_all(jnp.broadcast_to(lam, parts.shape), both, 0, 0, tiled=True)  4.51 us
  transfers between devices with their start and end apart: 5, of which 3 were waited for; matrix products, arithmetic and copies ran while one was open for 3% of the time, Pallas kernels for 9%

profile of v4, /device:TPU:1, one launch (start us, length us, event | category | flops | bytes accessed | tf_op | source)
XLA Modules:
  0.0 111.3 jit_solution(15484616432100129956)
XLA Ops:
  0.0 0.0 copy-start
  0.0 2.8 %shard_map.64 = bf16[2,64,24,128]{3,2,1,0:T(8,128)(2,1)} custom-call(s32[4]{0:T(128)} %owners_ref.5, bf16[4,60,24,128]{3,2,1,0:T(8,128)(2,1)} %bitcast.20), custom_call_target="tpu_custom_call" | custom-call | tf_op jit(solution)/shard_map/pallas_call | solution.py:45
  2.8 11.5 %all-to-all-start.1 = ((bf16[128,24,128]{2,1,0:T(8,128)(2,1)}), bf16[128,24,128]{2,1,0:T(8,128)(2,1)S(1)}, u32[]{:S(2)}, u32[]{:S(2)}) async-start(bf16[128,24,128]{2,1,0:T(8,128)(2,1)} %bitcast.22), calls=%async_computation.1 | async-start | bytes 1572864 | tf_op jit(solution)/shard_map/all_to_all | solution.py:293
  14.3 0.0 copy-done
  14.3 0.0 copy-start.1
  14.3 0.6 copy-done.1
  14.9 0.0 copy-start.2
  15.0 8.6 %shard_map.65 = (bf16[2,256,768]{2,1,0:T(8,128)(2,1)S(1)}, bf16[2880,768]{1,0:T(8,128)(2,1)}, s32[1]{0:T(128)}) custom-call(s32[4]{0:T(128)} %owners_ref.5, s32[2]{0:T(128)S(1)} %copy-done.1, bf16[2880,256]{1,0:T(8,128)(2,1)S(1)} %copy-done, bf16[2,2880,768]{2,1,0:T(8,128)(2,1)} %bitcast.19, bf16[2,2880,768]{2,1,0:T(8,128)(2,1)} %bitcast.18), custom_call_target="tpu_custom_call" | custom-call | flops 2264924160 | bytes 17694720 | tf_op jit(solution)/shard_map/pallas_call | solution.py:125
  24.2 6.1 %all-to-all-done.1 = bf16[128,24,128]{2,1,0:T(8,128)(2,1)S(1)} async-done(((bf16[128,24,128]{2,1,0:T(8,128)(2,1)}), bf16[128,24,128]{2,1,0:T(8,128)(2,1)S(1)}, u32[]{:S(2)}, u32[]{:S(2)}) %all-to-all-start.1) | async-done | bytes 786464 | tf_op jit(solution)/shard_map/all_to_all | solution.py:293
  30.3 0.0 copy-done.2
  30.3 0.8 shard_map.66
  31.1 0.0 slice-start
  31.1 28.4 %all_to_all.24.basis_ref = bf16[64,2,48,128]{3,2,1,0:T(8,128)(2,1)S(1)} all-to-all(bf16[64,2,48,128]{3,2,1,0:T(8,128)(2,1)S(1)} %shard_map.66), channel_id=1, replica_groups=mesh['basis'=64,'ex'=2] {'basis'}, dimensions={0} | all-to-all | bytes 3145728 | tf_op jit(solution)/shard_map/all_to_all | solution.py:309
  59.6 0.0 slice-start.1
  59.6 2.1 %collective-permute-start = (bf16[64,2,48,128]{3,2,1,0:T(8,128)(2,1)S(1)}, bf16[64,2,48,128]{3,2,1,0:T(8,128)(2,1)S(1)}, u32[]{:S(2)}, u32[]{:S(2)}) collective-permute-start(bf16[64,2,48,128]{3,2,1,0:T(8,128)(2,1)S(1)} %all_to_all.24.basis_ref), channel_id=1, source_target_pairs={{0,1},{1,0},{2,3},{3,2},{4,5},{5,4},{6,7},{7,6},{8,9},{9,8},{10,11... | collective-permute-start | bytes 4718600 | tf_op jit(solution)/shard_map/ppermute | solution.py:312
  61.7 2.5 %slice_bitcast_fusion.refs_1_ = bf16[2880,768]{1,0:T(8,128)(2,1)S(1)} fusion(bf16[2,768,2880]{1,2,0:T(8,128)(2,1)} %param.8), kind=kLoop, calls=%fused_computation.1 | loop fusion | bytes 8847360 | tf_op jit(solution)/shard_map/transpose | solution.py:299
  64.2 0.0 slice-done
  64.2 0.0 slice-done.1
  64.3 1.7 %shard_map.67 = (f32[256,256]{1,0:T(8,128)S(1)}, bf16[256,2880]{1,0:T(8,128)(2,1)S(1)}) custom-call(bf16[2880,768]{1,0:T(8,128)(2,1)S(1)} %bitcast.16, bf16[2,256,768]{2,1,0:T(8,128)(2,1)S(1)} %get-tuple-element.29.rg_ref.refs_2_, bf16[64,2,48,128]{3,2,1,0:T(8,128)(2,1)S(1)} %all_to_all.24.basis_ref), custom_call_target="tpu_custom_call" | custom-call | flops 1132462080 | bytes 4423680 | tf_op jit(solution)/shard_map/pallas_call | solution.py:210
  66.0 0.0 collective-permute-done.refs_4_
  66.0 5.8 %shard_map.68 = (f32[2,2,128,256]{3,2,1,0:T(8,128)}, f32[2,2,128,256]{3,2,1,0:T(8,128)}, f32[128,8,128]{2,1,0:T(8,128)}) custom-call(bf16[2880,768]{1,0:T(8,128)(2,1)S(1)} %bitcast.16, bf16[2880,768]{1,0:T(8,128)(2,1)S(1)} %slice_bitcast_fusion.refs_1_, bf16[2,256,768]{2,1,0:T(8,128)(2,1)S(1)} %get-tuple-element.29.rg_ref.refs_2_, ...), custom_call_target="tpu_custom_call" | custom-call | flops 3397386240 | bytes 13271040 | tf_op jit(solution)/shard_map/pallas_call | solution.py:219
  71.8 3.9 %all-to-all-start.3 = ((f32[128,8,128]{2,1,0:T(8,128)}), f32[128,8,128]{2,1,0:T(8,128)S(1)}, u32[]{:S(2)}, u32[]{:S(2)}) async-start(f32[128,8,128]{2,1,0:T(8,128)} %get-tuple-element.35), calls=%async_computation.3 | async-start | bytes 1048576 | tf_op jit(solution)/shard_map/all_to_all | solution.py:316
  75.7 1.1 %collective-permute-start.1 = (f32[2,2,128,256]{3,2,1,0:T(8,128)}, f32[2,2,128,256]{3,2,1,0:T(8,128)S(1)}, u32[]{:S(2)}, u32[]{:S(2)}) collective-permute-start(f32[2,2,128,256]{3,2,1,0:T(8,128)} %get-tuple-element.37), channel_id=1, source_target_pairs={{0,1},{1,0},{2,3},{3,2},{4,5},{5,4},{6,7},{7,6},{8,9},{9,8},{10,11... | collective-permute-start | bytes 1572872 | tf_op jit(solution)/shard_map/ppermute | solution.py:314
  76.8 12.6 %all-to-all-done.3 = f32[128,8,128]{2,1,0:T(8,128)S(1)} async-done(((f32[128,8,128]{2,1,0:T(8,128)}), f32[128,8,128]{2,1,0:T(8,128)S(1)}, u32[]{:S(2)}, u32[]{:S(2)}) %all-to-all-start.3) | async-done | bytes 524320 | tf_op jit(solution)/shard_map/all_to_all | solution.py:316
  89.4 0.1 reduce_sum.9
  89.6 0.8 broadcast_in_dim.2
  90.4 4.5 %all-to-all-start.4 = ((f32[128,8,128]{2,1,0:T(8,128)}), f32[128,8,128]{2,1,0:T(8,128)S(1)}, u32[]{:S(2)}, u32[]{:S(2)}) async-start(f32[128,8,128]{2,1,0:T(8,128)} %broadcast_in_dim.2), calls=%async_computation.4 | async-start | bytes 1048576 | tf_op jit(solution)/shard_map/all_to_all | solution.py:318
  94.9 0.0 collective-permute-done.1.got_ref
  94.9 13.7 %all-to-all-done.4.lam_ref = f32[128,8,128]{2,1,0:T(8,128)S(1)} async-done(((f32[128,8,128]{2,1,0:T(8,128)}), f32[128,8,128]{2,1,0:T(8,128)S(1)}, u32[]{:S(2)}, u32[]{:S(2)}) %all-to-all-start.4) | async-done | bytes 524320 | tf_op jit(solution)/shard_map/all_to_all | solution.py:318
  108.6 2.6 %shard_map.69 = f32[4,128,512]{2,1,0:T(8,128)} custom-call(f32[128,8,128]{2,1,0:T(8,128)S(1)} %all-to-all-done.4.lam_ref, f32[2,2,128,256]{3,2,1,0:T(8,128)} %get-tuple-element.36.keep_ref, f32[2,2,128,256]{3,2,1,0:T(8,128)S(1)} %collective-permute-done.1.got_ref), custom_call_target="tpu_custom_call" | custom-call | tf_op jit(solution)/shard_map/pallas_call | solution.py:272
  (4 shorter events, 0.0 us)
Async XLA Ops:
  0.0 14.3 %copy-start = (bf16[2880,256]{1,0:T(8,128)(2,1)S(1)}, bf16[2880,256]{1,0:T(8,128)(2,1)}, u32[]{:S(2)}) copy-start(bf16[2880,256]{1,0:T(8,128)(2,1)} %basis_ref.1) | copy-start | bytes 4423684
  2.8 27.5 %all-to-all-start.1 = ((bf16[128,24,128]{2,1,0:T(8,128)(2,1)}), bf16[128,24,128]{2,1,0:T(8,128)(2,1)S(1)}, u32[]{:S(2)}, u32[]{:S(2)}) async-start(bf16[128,24,128]{2,1,0:T(8,128)(2,1)} %bitcast.22), calls=%async_computation.1 | async-start | bytes 1572864 | tf_op jit(solution)/shard_map/all_to_all | solution.py:293
  14.3 0.7 copy-start.1
  14.9 15.3 %copy-start.2 = (s32[4]{0:T(128)S(1)}, s32[4]{0:T(128)}, u32[]{:S(2)}) copy-start(s32[4]{0:T(128)} %owners_ref.5) | copy-start | bytes 52
  31.1 33.1 %slice-start = ((s8[4423680]{0:T(1024)(128)(4,1)}), s8[4194304]{0:T(1024)(128)(4,1)S(1)}, s32[]{:S(2)}) async-start(s8[4423680]{0:T(1024)(128)(4,1)} %bitcast.15), calls=%async_computation.5 | async-start | bytes 8388608
  59.6 4.7 %slice-start.1 = ((s8[4423680]{0:T(1024)(128)(4,1)}), s8[229376]{0:T(1024)(128)(4,1)S(1)}, s32[]{:S(2)}) async-start(s8[4423680]{0:T(1024)(128)(4,1)} %bitcast.15), calls=%async_computation.6 | async-start | bytes 458752
  59.6 6.4 %collective-permute-start = (bf16[64,2,48,128]{3,2,1,0:T(8,128)(2,1)S(1)}, bf16[64,2,48,128]{3,2,1,0:T(8,128)(2,1)S(1)}, u32[]{:S(2)}, u32[]{:S(2)}) collective-permute-start(bf16[64,2,48,128]{3,2,1,0:T(8,128)(2,1)S(1)} %all_to_all.24.basis_ref), channel_id=1, source_target_pairs={{0,1},{1,0},{2,3},{3,2},{4,5},{5,4},{6,7},{7,6},{8,9},{9,8},{10,11... | collective-permute-start | bytes 4718600 | tf_op jit(solution)/shard_map/ppermute | solution.py:312
  71.8 17.6 %all-to-all-start.3 = ((f32[128,8,128]{2,1,0:T(8,128)}), f32[128,8,128]{2,1,0:T(8,128)S(1)}, u32[]{:S(2)}, u32[]{:S(2)}) async-start(f32[128,8,128]{2,1,0:T(8,128)} %get-tuple-element.35), calls=%async_computation.3 | async-start | bytes 1048576 | tf_op jit(solution)/shard_map/all_to_all | solution.py:316
  75.7 19.2 %collective-permute-start.1 = (f32[2,2,128,256]{3,2,1,0:T(8,128)}, f32[2,2,128,256]{3,2,1,0:T(8,128)S(1)}, u32[]{:S(2)}, u32[]{:S(2)}) collective-permute-start(f32[2,2,128,256]{3,2,1,0:T(8,128)} %get-tuple-element.37), channel_id=1, source_target_pairs={{0,1},{1,0},{2,3},{3,2},{4,5},{5,4},{6,7},{7,6},{8,9},{9,8},{10,11... | collective-permute-start | bytes 1572872 | tf_op jit(solution)/shard_map/ppermute | solution.py:314
  90.4 18.2 %all-to-all-start.4 = ((f32[128,8,128]{2,1,0:T(8,128)}), f32[128,8,128]{2,1,0:T(8,128)S(1)}, u32[]{:S(2)}, u32[]{:S(2)}) async-start(f32[128,8,128]{2,1,0:T(8,128)} %broadcast_in_dim.2), calls=%async_computation.4 | async-start | bytes 1048576 | tf_op jit(solution)/shard_map/all_to_all | solution.py:318
